TPU v7x, 128 devices: a whole 4x4x4 slice. The times are simulated.
128 devices in a mesh: store: 8 (over y, core), batch: 16 (over z, x).
Axes of the slice: x: 4, y: 4, z: 4, core: 2. Of those that a mesh axis runs over, the one named last changes fastest.
Arguments:
- features: bfloat16 [8, 128, 128, 512], P('store', 'batch'), may hold values from -6 to 6
- diag_blocks: bfloat16 [8, 128, 128, 128], P('store', 'batch'), may hold values from 0 to 0.015625
- coupling_blocks: bfloat16 [8, 128, 128, 128], P('store', 'batch'), may hold values from 0 to 0.0078125
- neighbour: int32 [8, 128], P('store', 'batch'), may hold values from 0 to 127, as said below
- assignment: int32 [8, 128], P('store', 'batch'), may hold values from 0 to 15, as said below
- feature_drop: int32 [8, 128, 2, 512], P('store', 'batch'), may hold values 0 or 1
- edge_drop: int32 [8, 128, 2, 128], P('store', 'batch'), may hold values 0 or 1
- weights: bfloat16 [2, 512, 512], replicated, may hold values from -0.25 to 0.25
Outputs:
- weight_grads: float32 [2, 512, 512], replicated
Inputs may be any that keep to these rules, and one draw needn't show every extreme that they name: `assignment`: within a group, the 8 clusters of one device (consecutive indices) go to distinct batches; in every group some batch receives one cluster from every device. neighbour[g, c] is a cluster of the same group with the same assignment as c, possibly c itself.
All inputs are finite; a program needn't handle non-finite values. No bound on the sum of `feature_drop` or of `edge_drop` on one device may be relied on, other than what follows from the above.
Results may differ from a plain program's by a relative error of at most 0.0025.
Values may be sent and summed in bfloat16 or wider, within the bound.
No kernel may reach another device: no remote copies, remote signals or barrier semaphores. Data moves between devices by JAX's collectives and lax.ppermute only.
A program may use at most 128 MiB of HBM per device.

v0:
```python
import jax
import jax.numpy as jnp
from jax import lax
from jax.sharding import PartitionSpec as P

SOFTMAX_TEMPER = 0.5
EPSILON = 1e-05


def local(
    features, diag_blocks, coupling_blocks, neighbour, assignment, feature_drop, edge_drop, weights
):
    count_of_slots = lax.axis_size("batch")
    owned = features.shape[1]
    node_count = features.shape[2]
    feature_columns = features.shape[3]
    layer_total = weights.shape[0]
    blocks = features[0]
    first_id = lax.axis_index("batch") * owned
    local_ids = first_id + jnp.arange(owned, dtype=jnp.int32)
    targets = jnp.arange(count_of_slots, dtype=jnp.int32)
    picks = assignment[0][None, :] == targets[:, None]
    chooser = picks.astype(jnp.bfloat16)
    present = jnp.any(picks, axis=1)
    sent_ids = jnp.where(present, jnp.sum(jnp.where(picks, local_ids[None, :], 0), axis=1), -1)
    sent_nbrs = jnp.where(present, jnp.sum(jnp.where(picks, neighbour[0][None, :], 0), axis=1), -1)
    labels = jnp.stack([sent_ids, sent_nbrs], axis=1).astype(jnp.bfloat16)

    def route_rows(values):
        return jnp.einsum(
            "dk,k...->d...", chooser, values, preferred_element_type=jnp.float32
        ).astype(jnp.bfloat16)

    feature_keep = feature_drop[0].astype(jnp.bfloat16)
    edge_keep = edge_drop[0].astype(jnp.bfloat16)
    arrived, adjacency, couplings, feature_slots, edge_slots, slot_labels = (
        lax.all_to_all(route_rows(blocks), "batch", split_axis=0, concat_axis=0, tiled=True),
        lax.all_to_all(
            route_rows(diag_blocks[0]), "batch", split_axis=0, concat_axis=0, tiled=True
        ),
        lax.all_to_all(
            route_rows(coupling_blocks[0]), "batch", split_axis=0, concat_axis=0, tiled=True
        ),
        lax.all_to_all(route_rows(feature_keep), "batch", split_axis=0, concat_axis=0, tiled=True),
        lax.all_to_all(route_rows(edge_keep), "batch", split_axis=0, concat_axis=0, tiled=True),
        lax.all_to_all(labels, "batch", split_axis=0, concat_axis=0, tiled=True),
    )
    first_inputs = arrived[None] * jnp.transpose(feature_slots, (1, 0, 2))[:, :, None, :]
    first_proj = jnp.einsum(
        "vsxf,fg->vsxg", first_inputs, weights[0], preferred_element_type=jnp.float32
    ).astype(jnp.bfloat16)
    edge_views = jnp.transpose(edge_slots, (1, 0, 2))[:, :, :, None]
    slot_ids = slot_labels[:, 0]
    slot_nbrs = slot_labels[:, 1]
    occupied = slot_ids >= 0
    linked_nodes = (slot_nbrs[:, None] == slot_ids[None, :]) & occupied[:, None] & occupied[None, :]
    link_half = linked_nodes.astype(jnp.bfloat16)
    link_full = linked_nodes.astype(jnp.float32)
    stored_inputs = []
    stored_pre = []
    projected = first_proj
    layer_inputs = first_inputs
    summed = None
    for layer_index in range(layer_total):
        if layer_index > 0:
            projected = jnp.einsum(
                "vsxf,fg->vsxg",
                layer_inputs,
                weights[layer_index],
                preferred_element_type=jnp.float32,
            ).astype(jnp.bfloat16)
        messages = projected * edge_views
        borrowed = jnp.einsum(
            "cs,vsxf->vcxf", link_half, messages, preferred_element_type=jnp.float32
        ).astype(jnp.bfloat16)
        own_part = jnp.einsum(
            "cxy,vcyf->vcxf", adjacency, messages, preferred_element_type=jnp.float32
        )
        summed = own_part + jnp.einsum(
            "cxy,vcyf->vcxf", couplings, borrowed, preferred_element_type=jnp.float32
        )
        stored_inputs.append(layer_inputs)
        stored_pre.append(summed)
        layer_inputs = jnp.maximum(summed, 0.0).astype(jnp.bfloat16)
    pooled = jnp.mean(jnp.maximum(summed, 0.0), axis=2)
    inv_norm = lax.rsqrt(jnp.mean(pooled * pooled, axis=-1) + EPSILON)
    unit_vecs = pooled * inv_norm[..., None]
    scale_factor = 1.0 / (feature_columns * SOFTMAX_TEMPER)
    scores = jnp.dot(unit_vecs[0], unit_vecs[1].T, precision=lax.Precision.HIGHEST) * scale_factor
    occupied_f = occupied.astype(jnp.float32)
    weighted = jnp.exp(scores) * occupied_f[None, :]
    totals = jnp.where(occupied, jnp.sum(weighted, axis=1), 1.0)
    coeffs = (weighted / totals[:, None] - jnp.eye(count_of_slots, dtype=jnp.float32)) * occupied_f[
        :, None
    ]
    unit_grad = (
        jnp.stack(
            [
                jnp.dot(coeffs, unit_vecs[1], precision=lax.Precision.HIGHEST),
                jnp.dot(coeffs.T, unit_vecs[0], precision=lax.Precision.HIGHEST),
            ]
        )
        * scale_factor
    )
    pooled_grad = (
        inv_norm[..., None] * unit_grad
        - (inv_norm**3 * jnp.sum(pooled * unit_grad, axis=-1) / feature_columns)[..., None] * pooled
    )
    pre_grad = (pooled_grad / node_count)[:, :, None, :] * (summed > 0).astype(jnp.float32)
    gradients = [None] * layer_total
    proj_grad = None
    for layer_index in reversed(range(layer_total)):
        rounded = pre_grad.astype(jnp.bfloat16)
        spread = jnp.einsum(
            "cxy,vcxf->vcyf", couplings, rounded, preferred_element_type=jnp.float32
        )
        message_grad = jnp.einsum(
            "cxy,vcxf->vcyf", adjacency, rounded, preferred_element_type=jnp.float32
        )
        message_grad = message_grad + jnp.einsum(
            "cs,vcyf->vsyf", link_full, spread, precision=lax.Precision.HIGHEST
        )
        proj_grad = (message_grad * edge_views).astype(jnp.bfloat16)
        if layer_index > 0:
            layer_grad = jnp.einsum(
                "vsxf,vsxg->fg",
                stored_inputs[layer_index],
                proj_grad,
                preferred_element_type=jnp.float32,
            )
            gradients[layer_index] = layer_grad
            hidden_grad = jnp.einsum(
                "vsxg,fg->vsxf", proj_grad, weights[layer_index], preferred_element_type=jnp.float32
            )
            pre_grad = hidden_grad * (stored_pre[layer_index - 1] > 0).astype(jnp.float32)
    first_grad = jnp.einsum(
        "vsxf,vsxg->fg", first_inputs, proj_grad, preferred_element_type=jnp.float32
    )
    gradients[0] = first_grad
    result = lax.psum(jnp.stack(gradients), ("store", "batch"))
    return result


def solution(mesh):
    return jax.shard_map(
        local,
        mesh=mesh,
        in_specs=(
            P("store", "batch", None, None),
            P("store", "batch", None, None),
            P("store", "batch", None, None),
            P("store", "batch"),
            P("store", "batch"),
            P("store", "batch", None, None),
            P("store", "batch", None, None),
            P(),
        ),
        out_specs=P(),
        check_vma=False,
    )
```

profile of v0, /device:TPU:1, one launch (start us, length us, event | category | flops | bytes accessed | tf_op | source)
XLA Modules:
  0.0 437.3 jit_solution(11566862781695039883)
XLA Ops:
  6.5 0.8 fusion.67
  7.4 0.8 select_reduce_fusion.1
  8.9 8.4 %all-to-all-start.4 = ((bf16[16,1,2]{2,1,0:T(2,128)(2,1)}), bf16[16,1,2]{2,1,0:T(2,128)(2,1)S(1)}, u32[]{:S(2)}, u32[]{:S(2)}) async-start(bf16[16,1,2]{2,1,0:T(2,128)(2,1)} %copy.46), calls=%async_computation.4 | async-start | bytes 16384 | tf_op jit(solution)/shard_map/all_to_all | solution.py:46
  17.3 0.7 convert_bitcast_fusion.1
  18.0 0.9 convolution_convert_fusion.4
  19.5 4.1 all-to-all-done.4
  23.6 3.4 all-to-all-start.2
  27.1 1.6 convolution_convert_fusion
  28.7 2.5 copy.35
  31.2 2.1 all-to-all-done.2
  33.2 4.5 %all-to-all-start = ((bf16[16,128,512]{2,1,0:T(8,128)(2,1)}), bf16[16,128,512]{2,1,0:T(8,128)(2,1)S(1)}, u32[]{:S(2)}, u32[]{:S(2)}) async-start(bf16[16,128,512]{2,1,0:T(8,128)(2,1)} %copy.35), calls=%async_computation | async-start | bytes 4194304 | tf_op jit(solution)/shard_map/all_to_all | solution.py:37
  39.1 0.9 copy.49
  40.5 0.9 copy.44
  41.5 21.7 %all-to-all-done = bf16[16,128,512]{2,1,0:T(8,128)(2,1)S(1)} async-done(((bf16[16,128,512]{2,1,0:T(8,128)(2,1)}), bf16[16,128,512]{2,1,0:T(8,128)(2,1)S(1)}, u32[]{:S(2)}, u32[]{:S(2)}) %all-to-all-start) | async-done | bytes 2097184 | tf_op jit(solution)/shard_map/all_to_all | solution.py:37
  63.3 7.7 %all-to-all-start.1 = ((bf16[16,2,512]{2,1,0:T(2,128)(2,1)}), bf16[16,2,512]{2,1,0:T(2,128)(2,1)S(1)}, u32[]{:S(2)}, u32[]{:S(2)}) async-start(bf16[16,2,512]{2,1,0:T(2,128)(2,1)} %copy.38), calls=%async_computation.1 | async-start | bytes 65536 | tf_op jit(solution)/shard_map/all_to_all | solution.py:44
  71.0 2.4 copy.36
  73.4 4.0 all-to-all-done.1
  77.5 3.6 all-to-all-start.3
  81.0 7.1 %convert_multiply_fusion.1 = bf16[2,16,128,512]{3,2,1,0:T(8,128)(2,1)S(1)} fusion(bf16[2,16,128]{2,1,0:T(8,128)(2,1)S(1)} %copy.42, bf16[2,512,512]{2,1,0:T(8,128)(2,1)} %param.15, bf16[2,16,512]{2,0,1:T(2,128)(2,1)S(1)} %bitcast.183, bf16[16,128,512]{1,2,0:T(8,128)(2,1)} %copy.36), kind=kOutput, calls=%fused_computation.34 | convolution fusion | flops 2153775104 | bytes 6856704 | tf_op jit(solution)/shard_map/vsxf,fg->vsxg/dot_general | solution.py:49
  88.2 2.0 copy-done.4
  90.1 4.8 %fusion.22 = bf16[2,128,512,16]{2,3,1,0:T(8,128)(2,1)} fusion(bf16[2,16,128,512]{3,2,1,0:T(8,128)(2,1)S(1)} %convert_multiply_fusion.1, pred[16]{0:T(512)(128)(4,1)S(1)} %get-tuple-element.12, pred[16]{0:T(512)(128)(4,1)S(1)} %get-tuple-element.10, bf16[16]{0:T(256)(128)(2,1)S(1)} %get-tuple-element.14, bf16[16]{0:T(256)(128)(2,1)S(1)} %get-tuple-element.13), kind=kOutput, calls=%fused_computation.27 | convolution fusion | flops 67110144 | bytes 8388704 | tf_op jit(solution)/shard_map/cs,vsxf->vcxf/dot_general | solution.py:73
  94.9 7.9 %copy.67 = bf16[2,128,512,16]{1,2,0,3:T(8,128)(2,1)} copy(bf16[2,128,512,16]{2,3,1,0:T(8,128)(2,1)} %fusion.22) | data formatting | bytes 8388608 | tf_op jit(solution)/shard_map/cs,vsxf->vcxf/dot_general | solution.py:73
  102.8 6.6 %all-to-all-start.5 = ((bf16[16,128,128]{2,1,0:T(8,128)(2,1)}), bf16[16,128,128]{2,1,0:T(8,128)(2,1)S(1)}, u32[]{:S(2)}, u32[]{:S(2)}) async-start(bf16[16,128,128]{2,1,0:T(8,128)(2,1)} %copy.49), calls=%async_computation.5 | async-start | bytes 1048576 | tf_op jit(solution)/shard_map/all_to_all | solution.py:41
  109.4 11.8 %all-reduce.2.cloned.1.call-start = ((), (), s32[]{:S(2)}) async-start(), calls=%async_computation.6 | async-start | bytes 4194304 | tf_op jit(solution)/shard_map/psum | solution.py:140
  121.2 6.8 %fusion.16 = f32[16,2,512,128]{3,2,1,0:T(8,128)} fusion(bf16[2,16,128,512]{3,2,1,0:T(8,128)(2,1)} %copy-done.4, bf16[16,128,128]{2,1,0:T(8,128)(2,1)S(1)} %all-to-all-done.3), kind=kOutput, calls=%fused_computation.21 | convolution fusion | flops 536870912 | bytes 13107200 | tf_op jit(solution)/shard_map/cxy,vcyf->vcxf/dot_general | solution.py:76
  127.9 6.7 %fusion.14 = f32[16,2,512,128]{3,2,1,0:T(8,128)} fusion(bf16[2,128,512,16]{1,2,0,3:T(8,128)(2,1)} %copy.67, bf16[16,128,128]{2,1,0:T(8,128)(2,1)S(1)} %all-to-all-done.5), kind=kOutput, calls=%fused_computation.19 | convolution fusion | flops 536870912 | bytes 13107200 | tf_op jit(solution)/shard_map/cxy,vcyf->vcxf/dot_general | solution.py:79
  134.6 7.3 %fusion.6 = bf16[2,16,128,512]{2,3,0,1:T(8,128)(2,1)S(1)} fusion(f32[16,2,512,128]{3,2,1,0:T(8,128)} %fusion.16, f32[16,2,512,128]{3,2,1,0:T(8,128)} %fusion.14), kind=kLoop, calls=%fused_computation.13 | loop fusion | flops 6291456 | bytes 20971520 | tf_op jit(solution)/shard_map/convert_element_type | solution.py:84
  141.9 2.6 convert_multiply_fusion
  144.6 2.9 fusion.20
  147.5 4.6 %fusion.8 = f32[16,2,512,128]{3,2,1,0:T(8,128)S(1)} fusion(bf16[2,128,512,16]{2,3,1,0:T(8,128)(2,1)S(1)} %fusion.20, bf16[16,128,128]{2,1,0:T(8,128)(2,1)S(1)} %all-to-all-done.5), kind=kOutput, calls=%fused_computation.15 | convolution fusion | flops 536870912 | bytes 13107200 | tf_op jit(solution)/shard_map/cxy,vcyf->vcxf/dot_general | solution.py:79
  152.1 8.7 %maximum_reduce_fusion = (f32[16,2,512]{2,1,0:T(2,128)S(1)}, f32[16,2,512,128]{3,2,1,0:T(8,128)}) fusion(f32[16,2,512,128]{3,2,1,0:T(8,128)S(1)} %fusion.8, bf16[16,128,128]{2,1,0:T(8,128)(2,1)S(1)} %all-to-all-done.3, bf16[2,16,128,512]{3,2,1,0:T(8,128)(2,1)} %copy-done.5), kind=kOutput, calls=%fused_computation.11 | convolution fusion | flops 543145984 | bytes 21561344 | tf_op jit(solution)/shard_map/cxy,vcyf->vcxf/dot_general | solution.py:76
  161.9 5.4 %select_convert_fusion.1 = bf16[2,16,128,512]{2,3,0,1:T(8,128)(2,1)S(1)} fusion(bf16[2,16,512]{2,0,1:T(2,128)(2,1)S(1)} %copy.55, f32[16,2,512,128]{3,2,1,0:T(8,128)} %get-tuple-element.18, f32[16,2,512,128]{3,2,1,0:T(8,128)S(1)} %fusion.8), kind=kLoop, calls=%fused_computation.10 | loop fusion | flops 6291456 | bytes 21004288 | tf_op jit(solution)/shard_map/convert_element_type | solution.py:113
  167.3 1.9 copy-done.2
  169.3 4.5 %fusion.44 = f32[16,2,512,128]{3,2,1,0:T(8,128)} fusion(bf16[2,16,128,512]{2,3,0,1:T(8,128)(2,1)S(1)} %select_convert_fusion.1, bf16[16,128,128]{2,1,0:T(8,128)(2,1)S(1)} %all-to-all-done.5), kind=kOutput, calls=%fused_computation.56 | convolution fusion | flops 536870912 | bytes 13107200 | tf_op jit(solution)/shard_map/cxy,vcxf->vcyf/dot_general | solution.py:114
  173.7 10.3 %copy.75 = f32[16,2,512,128]{2,0,3,1:T(8,128)} copy(f32[16,2,512,128]{3,2,1,0:T(8,128)} %fusion.44) | data formatting | bytes 16777216 | tf_op jit(solution)/shard_map/cxy,vcxf->vcyf/dot_general | solution.py:114
  184.1 11.4 %fusion.4 = f32[2,128,512,16]{2,3,1,0:T(8,128)} fusion(f32[16,2,512,128]{2,0,3,1:T(8,128)} %copy.75, pred[16]{0:T(512)(128)(4,1)S(1)} %get-tuple-element.12, pred[16]{0:T(512)(128)(4,1)S(1)} %get-tuple-element.10, bf16[16]{0:T(256)(128)(2,1)S(1)} %get-tuple-element.14, bf16[16]{0:T(256)(128)(2,1)S(1)} %get-tuple-element.13), kind=kOutput, calls=%fused_computation.6 | convolution fusion | flops 402654464 | bytes 16777312 | tf_op jit(solution)/shard_map/cs,vcyf->vsyf/dot_general | solution.py:120
  195.5 10.4 %copy.56 = f32[2,128,512,16]{1,2,0,3:T(8,128)} copy(f32[2,128,512,16]{2,3,1,0:T(8,128)} %fusion.4) | data formatting | bytes 16777216 | tf_op jit(solution)/shard_map/cs,vcyf->vsyf/dot_general | solution.py:120
  205.9 5.9 %fusion.3 = bf16[2,16,128,512]{2,3,0,1:T(8,128)(2,1)S(1)} fusion(f32[2,128,512,16]{1,2,0,3:T(8,128)} %copy.56, f32[2,16,128]{2,0,1:T(2,128)S(1)} %bitcast_convert_fusion, bf16[2,16,128,512]{2,3,0,1:T(8,128)(2,1)} %copy-done.2, bf16[16,128,128]{2,1,0:T(8,128)(2,1)S(1)} %all-to-all-done.3), kind=kOutput, calls=%fused_computation.5 | convolution fusion | flops 543162368 | bytes 17317888 | tf_op jit(solution)/shard_map/cxy,vcxf->vcyf/dot_general | solution.py:117
  211.8 8.6 %select_convert_fusion = bf16[2,16,128,512]{2,3,0,1:T(8,128)(2,1)S(1)} fusion(f32[16,2,512,128]{3,2,1,0:T(8,128)} %fusion.16, f32[16,2,512,128]{3,2,1,0:T(8,128)} %fusion.14, bf16[2,16,128,512]{2,3,0,1:T(8,128)(2,1)S(1)} %fusion.3, bf16[2,512,512]{2,1,0:T(8,128)(2,1)S(1)} %copy-done.9), kind=kOutput, calls=%fused_computation.9 | convolution fusion | flops 2155872256 | bytes 25690112 | tf_op jit(solution)/shard_map/vsxg,fg->vsxf/dot_general | solution.py:132
  220.4 3.3 convolution_bitcast_fusion.1
  223.7 4.5 %convolution_bitcast_fusion = f32[2,16,128,512]{2,3,0,1:T(8,128)} fusion(bf16[2,16,128,512]{2,3,0,1:T(8,128)(2,1)S(1)} %select_convert_fusion, bf16[16,128,128]{2,1,0:T(8,128)(2,1)S(1)} %all-to-all-done.5), kind=kOutput, calls=%fused_computation.35 | convolution fusion | flops 536870912 | bytes 13107200 | tf_op jit(solution)/shard_map/cxy,vcxf->vcyf/dot_general | solution.py:114
  228.2 10.3 %copy.78 = f32[2,16,128,512]{3,1,2,0:T(8,128)} copy(f32[2,16,128,512]{2,3,0,1:T(8,128)} %convolution_bitcast_fusion) | data formatting | bytes 16777216 | tf_op jit(solution)/shard_map/cxy,vcxf->vcyf/transpose | solution.py:114
  238.5 11.4 %fusion.61 = f32[2,128,512,16]{2,3,1,0:T(8,128)} fusion(f32[2,16,128,512]{3,1,2,0:T(8,128)} %copy.78, pred[16]{0:T(512)(128)(4,1)S(1)} %get-tuple-element.12, pred[16]{0:T(512)(128)(4,1)S(1)} %get-tuple-element.10, bf16[16]{0:T(256)(128)(2,1)S(1)} %get-tuple-element.14, bf16[16]{0:T(256)(128)(2,1)S(1)} %get-tuple-element.13), kind=kOutput, calls=%fused_computation.83 | convolution fusion | flops 402654464 | bytes 16777312 | tf_op jit(solution)/shard_map/cs,vcyf->vsyf/dot_general | solution.py:120
  250.0 10.3 %copy.79 = f32[2,128,512,16]{1,2,0,3:T(8,128)} copy(f32[2,128,512,16]{2,3,1,0:T(8,128)} %fusion.61) | data formatting | bytes 16777216 | tf_op jit(solution)/shard_map/cs,vcyf->vsyf/dot_general | solution.py:120
  260.3 9.2 %fusion.34 = f32[1,512,512]{2,1,0:T(8,128)} fusion(f32[2,128,512,16]{1,2,0,3:T(8,128)} %copy.79, f32[2,16,128]{2,0,1:T(2,128)S(1)} %bitcast_convert_fusion, bf16[2,16,128,512]{2,3,0,1:T(8,128)(2,1)} %copy-done.3, bf16[16,128,128]{2,1,0:T(8,128)(2,1)S(1)} %all-to-all-done.3, bf16[2,16,512]{2,0,1:T(2,128)(2,1)S(1)} %bitcast.184, ...), kind=kOutput, calls=%fused_computation.40 | convolution fusion | flops 2692743168 | bytes 16302080 | tf_op jit(solution)/shard_map/vsxf,vsxg->fg/dot_general | solution.py:136
  269.5 3.1 pad_maximum_fusion
  272.6 154.6 %all-reduce.2.cloned.1.call-done = f32[2,512,512]{2,1,0:T(8,128)} async-done(((f32[2,512,512]{2,1,0:T(8,128)}), f32[2,512,512]{2,1,0:T(8,128)}) %all-reduce.2.cloned.1.call-update) | async-done | bytes 2097168 | tf_op jit(solution)/shard_map/psum | solution.py:140
  427.2 3.1 copy.124
  (56 shorter events, 4.3 us)
Async XLA Ops:
  6.5 20.5 %copy-start = (bf16[1,8,128,512]{3,2,1,0:T(8,128)(2,1)S(1)}, bf16[1,8,128,512]{3,2,1,0:T(8,128)(2,1)}, u32[]{:S(2)}) copy-start(bf16[1,8,128,512]{3,2,1,0:T(8,128)(2,1)} %param.8) | copy-start | bytes 3145732
  8.9 14.8 %all-to-all-start.4 = ((bf16[16,1,2]{2,1,0:T(2,128)(2,1)}), bf16[16,1,2]{2,1,0:T(2,128)(2,1)S(1)}, u32[]{:S(2)}, u32[]{:S(2)}) async-start(bf16[16,1,2]{2,1,0:T(2,128)(2,1)} %copy.46), calls=%async_computation.4 | async-start | bytes 16384 | tf_op jit(solution)/shard_map/all_to_all | solution.py:46
  23.6 9.6 %all-to-all-start.2 = ((bf16[16,2,128]{2,1,0:T(2,128)(2,1)}), bf16[16,2,128]{2,1,0:T(2,128)(2,1)S(1)}, u32[]{:S(2)}, u32[]{:S(2)}) async-start(bf16[16,2,128]{2,1,0:T(2,128)(2,1)} %copy.41), calls=%async_computation.2 | async-start | bytes 16384 | tf_op jit(solution)/shard_map/all_to_all | solution.py:45
  28.6 9.1 %copy-start.12 = (s32[1,8,2,512]{3,2,1,0:T(2,128)S(1)}, s32[1,8,2,512]{3,2,1,0:T(2,128)}, u32[]{:S(2)}) copy-start(s32[1,8,2,512]{3,2,1,0:T(2,128)} %param.13) | copy-start | bytes 98308
  28.6 9.2 %copy-start.13 = (s32[1,8]{1,0:T(1,128)S(1)}, s32[1,8]{1,0:T(1,128)}, u32[]{:S(2)}) copy-start(s32[1,8]{1,0:T(1,128)} %param.12) | copy-start | bytes 100
  28.7 10.1 %copy-start.10 = (bf16[1,8,128,128]{3,2,1,0:T(8,128)(2,1)S(1)}, bf16[1,8,128,128]{3,2,1,0:T(8,128)(2,1)}, u32[]{:S(2)}) copy-start(bf16[1,8,128,128]{3,2,1,0:T(8,128)(2,1)} %param.10) | copy-start | bytes 786436
  28.7 11.4 %copy-start.11 = (bf16[1,8,128,128]{3,2,1,0:T(8,128)(2,1)S(1)}, bf16[1,8,128,128]{3,2,1,0:T(8,128)(2,1)}, u32[]{:S(2)}) copy-start(bf16[1,8,128,128]{3,2,1,0:T(8,128)(2,1)} %param.9) | copy-start | bytes 786436
  33.2 30.0 %all-to-all-start = ((bf16[16,128,512]{2,1,0:T(8,128)(2,1)}), bf16[16,128,512]{2,1,0:T(8,128)(2,1)S(1)}, u32[]{:S(2)}, u32[]{:S(2)}) async-start(bf16[16,128,512]{2,1,0:T(8,128)(2,1)} %copy.35), calls=%async_computation | async-start | bytes 4194304 | tf_op jit(solution)/shard_map/all_to_all | solution.py:37
  63.3 14.2 %all-to-all-start.1 = ((bf16[16,2,512]{2,1,0:T(2,128)(2,1)}), bf16[16,2,512]{2,1,0:T(2,128)(2,1)S(1)}, u32[]{:S(2)}, u32[]{:S(2)}) async-start(bf16[16,2,512]{2,1,0:T(2,128)(2,1)} %copy.38), calls=%async_computation.1 | async-start | bytes 65536 | tf_op jit(solution)/shard_map/all_to_all | solution.py:44
  77.5 25.3 %all-to-all-start.3 = ((bf16[16,128,128]{2,1,0:T(8,128)(2,1)}), bf16[16,128,128]{2,1,0:T(8,128)(2,1)S(1)}, u32[]{:S(2)}, u32[]{:S(2)}) async-start(bf16[16,128,128]{2,1,0:T(8,128)(2,1)} %copy.44), calls=%async_computation.3 | async-start | bytes 1048576 | tf_op jit(solution)/shard_map/all_to_all | solution.py:38
  88.2 2.0 copy-start.4
  102.8 25.1 %all-to-all-start.5 = ((bf16[16,128,128]{2,1,0:T(8,128)(2,1)}), bf16[16,128,128]{2,1,0:T(8,128)(2,1)S(1)}, u32[]{:S(2)}, u32[]{:S(2)}) async-start(bf16[16,128,128]{2,1,0:T(8,128)(2,1)} %copy.49), calls=%async_computation.5 | async-start | bytes 1048576 | tf_op jit(solution)/shard_map/all_to_all | solution.py:41
  109.4 317.9 %all-reduce.2.cloned.1.call-start = ((), (), s32[]{:S(2)}) async-start(), calls=%async_computation.6 | async-start | bytes 4194304 | tf_op jit(solution)/shard_map/psum | solution.py:140
  134.6 7.3 %copy-start.9 = (bf16[2,512,512]{2,1,0:T(8,128)(2,1)S(1)}, bf16[2,512,512]{2,1,0:T(8,128)(2,1)}, u32[]{:S(2)}) copy-start(bf16[2,512,512]{2,1,0:T(8,128)(2,1)} %param.15) | copy-start | bytes 3145732
  141.9 2.6 copy-start.6
  144.6 2.9 copy-start.5
  167.3 2.0 copy-start.2
  211.8 8.6 %copy-start.7 = (bf16[2,16,128,512]{2,3,0,1:T(8,128)(2,1)S(1)}, bf16[2,16,128,512]{2,3,0,1:T(8,128)(2,1)}, u32[]{:S(2)}) copy-start(bf16[2,16,128,512]{2,3,0,1:T(8,128)(2,1)} %copy-done.6) | copy-start | bytes 12582916
  220.4 3.3 copy-start.3
  250.0 10.3 %copy-start.8 = (bf16[16,128,512]{1,2,0:T(8,128)(2,1)S(1)}, bf16[16,128,512]{1,2,0:T(8,128)(2,1)}, u32[]{:S(2)}) copy-start(bf16[16,128,512]{1,2,0:T(8,128)(2,1)} %copy.36) | copy-start | bytes 6291460
  269.5 160.8 %copy-start.1 = (bf16[1,8,128,512]{3,2,1,0:T(8,128)(2,1)S(1)}, bf16[1,8,128,512]{3,2,1,0:T(8,128)(2,1)}, u32[]{:S(2)}) copy-start(bf16[1,8,128,512]{3,2,1,0:T(8,128)(2,1)} %param.8) | copy-start | bytes 3145732
Sparse Core Ops, SparseCore 0:
  272.7 154.4 all-reduce.1
where the time goes:
time: 446 us; the launch traced here: 437 us
  waiting for transfers between devices  187 us (42%)
  matrix products  107 us (24%)
  local copies, waits for them, and re-layouts  65.1 us (15%)
  starting transfers between devices  46 us (10%)
  other arithmetic  18.6 us (4%)
  between operations  14 us (3%)
    psum x1, waiting for transfers between devices, local(): result = lax.psum(jnp.stack(gradients), ('store', 'batch'))  155 us
    dot_general x2, matrix products, local(): jnp.einsum('cs,vcyf->vsyf', link_full, spread, precision=lax.Precision.HI...  22.8 us
    all_to_all x1, waiting for transfers between devices, local(): lax.all_to_all(route_rows(blocks), 'batch', split_axis=0, concat_axis=0,...  21.7 us
    dot_general x2, local copies, waits for them, and re-layouts, local(): jnp.einsum('cs,vcyf->vsyf', link_full, spread, precision=lax.Precision.HI...  20.7 us
    dot_general x2, matrix products, local(): jnp.einsum('cxy,vcyf->vcxf', adjacency, messages, preferred_element_type=...  15.5 us
    psum x1, starting transfers between devices, local(): result = lax.psum(jnp.stack(gradients), ('store', 'batch'))  11.8 us
    dot_general x2, matrix products, local(): jnp.einsum('cxy,vcyf->vcxf', couplings, borrowed, preferred_element_type=...  11.3 us
    dot_general x1, local copies, waits for them, and re-layouts, local(): jnp.einsum('cxy,vcxf->vcyf', couplings, rounded, preferred_element_type=j...  10.3 us
  transfers between devices with their start and end apart: 7, of which 5 were waited for; matrix products, arithmetic and copies ran while one was open for 9% of the time, Pallas kernels for 0%

commit v1 on v0

v1 whole, which is shorter than its diff:
```python
import jax
import jax.numpy as jnp
from jax import lax
from jax.experimental import pallas as pl
from jax.experimental.pallas import tpu as pltpu
from jax.sharding import PartitionSpec as P

SOFTMAX_TEMPER = 0.5
EPSILON = 1e-05

LANES = 128
META = 16


def pack_kernel(
    assign, neighbour, features, diag, coupling, feature_drop, edge_drop, send, meta
):
    owned, nodes, columns = features.shape[1:]
    blocks = columns // LANES
    meta[...] = jnp.zeros_like(meta)
    for k in range(owned):
        target = assign[0, k]
        for j in range(blocks):
            send[target, pl.ds(j * nodes, nodes), :] = features[0, k, :, pl.ds(j * LANES, LANES)]
        send[target, pl.ds(blocks * nodes, nodes), :] = diag[0, k]
        send[target, pl.ds((blocks + 1) * nodes, nodes), :] = coupling[0, k]
        for v in range(2):
            for j in range(blocks):
                meta[target, v * blocks + j, :] = feature_drop[
                    0, k, v, pl.ds(j * LANES, LANES)
                ].astype(jnp.float32)
            meta[target, 2 * blocks + v, :] = edge_drop[0, k, v, :].astype(jnp.float32)
        slot = neighbour[0, k] // owned + 1
        meta[target, 2 * blocks + 2, :] = jnp.full((LANES,), slot, jnp.float32)
    send[:, pl.ds((blocks + 2) * nodes, META), :] = meta[...].astype(jnp.bfloat16)


def dot(a, b, contract, precision=None):
    return lax.dot_general(
        a, b, (contract, ((), ())), precision=precision, preferred_element_type=jnp.float32
    )


def step_kernel(
    core, weights, recv, out,
    rbuf, meta, slots, slot_ids, h0, p0, p1, h1, adj, active, acc, pooled,
    sems, meta_sem, slot_sem,
):
    count = recv.shape[0]
    columns = weights.shape[1]
    blocks = columns // LANES
    nodes = adj.shape[1]
    body = (blocks + 2) * nodes
    rows = 2 * nodes
    low = jnp.bfloat16

    meta_copy = pltpu.make_async_copy(recv.at[:, pl.ds(body, META), :], meta, meta_sem)
    meta_copy.start()
    for s in range(count):
        pltpu.make_async_copy(recv.at[s, pl.ds(0, body), :], rbuf.at[s], sems.at[s]).start()
    meta_copy.wait()
    slots[...] = meta[...].astype(jnp.float32)
    pooled[2, :, pl.ds(0, LANES)] = slots[:, 2 * blocks + 2, :]
    nbr = slots[:, 2 * blocks + 2, :].astype(jnp.int32) - 1
    own = lax.broadcasted_iota(jnp.int32, nbr.shape, 0)
    linked = jnp.where(nbr < 0, own, nbr)

    def put_ids(ids_vmem):
        ids_vmem[...] = linked
        copy = pltpu.make_async_copy(ids_vmem, slot_ids, slot_sem)
        copy.start()
        copy.wait()

    pl.run_scoped(put_ids, pltpu.VMEM((count, LANES), jnp.int32))

    def project(s, carry):
        pltpu.make_async_copy(recv.at[s, pl.ds(0, body), :], rbuf.at[s], sems.at[s]).wait()
        n = slot_ids[s, 0]
        own_rows = rbuf[s, pl.ds(0, blocks * nodes), :].reshape(blocks, nodes, LANES)
        diag = rbuf[s, pl.ds(blocks * nodes, nodes), :]
        coupling = rbuf[s, pl.ds((blocks + 1) * nodes, nodes), :]
        zero = jnp.zeros((), low)
        for v in range(2):
            pieces = []
            for j in range(blocks):
                keep = slots[s, pl.ds(v * blocks + j, 1), :] > 0.5
                pieces.append(jnp.where(keep, own_rows[j], zero))
            base = s * rows + v * nodes
            h0[pl.ds(base, nodes), :] = jnp.concatenate(pieces, axis=1)
            own_keep = slots[s, pl.ds(2 * blocks + v, 1), :] > 0.5
            far_keep = slots[n, pl.ds(2 * blocks + v, 1), :] > 0.5
            adj[2 * s + v] = jnp.concatenate(
                [jnp.where(own_keep, diag, zero), jnp.where(far_keep, coupling, zero)], axis=1
            )
        base = s * rows
        p0[pl.ds(base, rows), :] = dot(
            h0[pl.ds(base, rows), :], weights[0], ((1,), (0,))
        ).astype(low)
        acc[pl.ds(base, rows), :] = jnp.zeros((rows, columns), jnp.float32)
        return carry

    lax.fori_loop(0, count, project, 0)

    def gather(source, s, n, v):
        return dot(
            adj[2 * s + v],
            jnp.concatenate(
                [
                    source[pl.ds(s * rows + v * nodes, nodes), :],
                    source[pl.ds(n * rows + v * nodes, nodes), :],
                ],
                axis=0,
            ),
            ((1,), (0,)),
        )

    def first_layer(s, carry):
        n = slot_ids[s, 0]
        for v in range(2):
            h1[pl.ds(s * rows + v * nodes, nodes), :] = jnp.maximum(
                gather(p0, s, n, v), 0.0
            ).astype(low)
        p1[pl.ds(s * rows, rows), :] = dot(
            h1[pl.ds(s * rows, rows), :], weights[1], ((1,), (0,))
        ).astype(low)
        return carry

    lax.fori_loop(0, count, first_layer, 0)

    def second_layer(s, carry):
        n = slot_ids[s, 0]
        for v in range(2):
            summed = jnp.maximum(gather(p1, s, n, v), 0.0)
            active[pl.ds(s * rows + v * nodes, nodes), :] = jnp.where(
                summed > 0, 1.0, 0.0
            ).astype(low)
            pooled[v, pl.ds(s, 1), :] = jnp.sum(summed, axis=0, keepdims=True) * (1.0 / nodes)
        return carry

    lax.fori_loop(0, count, second_layer, 0)

    flags = jnp.where(pooled[2, :, pl.ds(0, LANES)] > 0.5, 1.0, 0.0)
    occ_col = flags[:, 0:1]
    occ_row = dot(
        jnp.full((8, LANES), 1.0 / LANES, jnp.float32), flags, ((1,), (1,)), lax.Precision.HIGHEST
    )[0:1, :]
    means = [pooled[0], pooled[1]]
    inv = [
        lax.rsqrt(jnp.mean(e * e, axis=-1, keepdims=True) + EPSILON) for e in means
    ]
    unit = [e * i for e, i in zip(means, inv)]
    scale = 1.0 / (columns * SOFTMAX_TEMPER)
    high = lax.Precision.HIGHEST
    scores = dot(unit[0], unit[1], ((1,), (1,)), high) * scale
    weighted = jnp.exp(scores) * occ_row
    totals = jnp.where(occ_col > 0.5, jnp.sum(weighted, axis=1, keepdims=True), 1.0)
    row_id = lax.broadcasted_iota(jnp.int32, (count, count), 0)
    col_id = lax.broadcasted_iota(jnp.int32, (count, count), 1)
    eye = jnp.where(row_id == col_id, 1.0, 0.0)
    coeffs = (weighted / totals - eye) * occ_col
    unit_grad = [
        dot(coeffs, unit[1], ((1,), (0,)), high) * scale,
        dot(coeffs, unit[0], ((0,), (0,)), high) * scale,
    ]
    for v in range(2):
        grad = (
            inv[v] * unit_grad[v]
            - (inv[v] ** 3 * jnp.sum(means[v] * unit_grad[v], axis=-1, keepdims=True) / columns)
            * means[v]
        )
        pooled[v] = (grad / nodes).astype(low).astype(jnp.float32)

    def scatter(s, v, grad):
        n = slot_ids[s, 0]
        spread = dot(adj[2 * s + v], grad, ((0,), (0,)))
        mine = pl.ds(s * rows + v * nodes, nodes)
        acc[mine, :] = acc[mine, :] + spread[:nodes]
        far = pl.ds(n * rows + v * nodes, nodes)
        acc[far, :] = acc[far, :] + spread[nodes:]

    def second_back(s, carry):
        for v in range(2):
            row = pooled[v, pl.ds(s, 1), :].astype(low)
            scatter(s, v, active[pl.ds(s * rows + v * nodes, nodes), :] * row)
        return carry

    lax.fori_loop(0, count, second_back, 0)

    keep_one = core[0] ^ 1
    keep_zero = core[0]
    chunk = 4 * rows
    out[...] = jnp.zeros_like(out)

    def second_weights(i, carry):
        span = pl.ds(i * chunk, chunk)
        grad = acc[span, :].astype(low)
        acc[span, :] = jnp.zeros((chunk, columns), jnp.float32)
        hidden = h1[span, :]
        out[keep_one] = out[keep_one] + dot(hidden, grad, ((0,), (0,)))
        below = dot(grad, weights[1], ((1,), (1,)))
        p0[span, :] = jnp.where(hidden > 0, below, 0.0).astype(low)
        return carry

    lax.fori_loop(0, count // 4, second_weights, 0)

    def first_back(s, carry):
        for v in range(2):
            scatter(s, v, p0[pl.ds(s * rows + v * nodes, nodes), :])
        return carry

    lax.fori_loop(0, count, first_back, 0)

    def first_weights(i, carry):
        span = pl.ds(i * chunk, chunk)
        out[keep_zero] = out[keep_zero] + dot(
            h0[span, :], acc[span, :].astype(low), ((0,), (0,))
        )
        return carry

    lax.fori_loop(0, count // 4, first_weights, 0)


def local(
    features, diag_blocks, coupling_blocks, neighbour, assignment, feature_drop, edge_drop, weights
):
    count = lax.axis_size("batch")
    stores = lax.axis_size("store")
    _, owned, nodes, columns = features.shape
    blocks = columns // LANES
    body = (blocks + 2) * nodes
    low = jnp.bfloat16
    smem = pl.BlockSpec(memory_space=pltpu.SMEM)
    vmem = pl.BlockSpec(memory_space=pltpu.VMEM)
    raw = pl.BlockSpec(memory_space=pl.ANY)
    send = pl.pallas_call(
        pack_kernel,
        out_shape=jax.ShapeDtypeStruct((count, body + META, LANES), low),
        in_specs=[smem, smem, vmem, vmem, vmem, vmem, vmem],
        out_specs=vmem,
        scratch_shapes=[pltpu.VMEM((count, META, LANES), jnp.float32)],
        name="pack",
    )(assignment, neighbour, features, diag_blocks, coupling_blocks, feature_drop, edge_drop)
    recv = lax.all_to_all(send, "batch", split_axis=0, concat_axis=0, tiled=True)
    parity = lax.axis_index("store") % 2
    total = count * 2 * nodes
    halves = pl.pallas_call(
        step_kernel,
        out_shape=jax.ShapeDtypeStruct((2, columns, columns), jnp.float32),
        in_specs=[smem, vmem, raw],
        out_specs=vmem,
        scratch_shapes=[
            pltpu.VMEM((count, body, LANES), low),
            pltpu.VMEM((count, META, LANES), low),
            pltpu.VMEM((count, META, LANES), jnp.float32),
            pltpu.SMEM((count, LANES), jnp.int32),
            pltpu.VMEM((total, columns), low),
            pltpu.VMEM((total, columns), low),
            pltpu.VMEM((total, columns), low),
            pltpu.VMEM((total, columns), low),
            pltpu.VMEM((2 * count, nodes, 2 * nodes), low),
            pltpu.VMEM((total, columns), low),
            pltpu.VMEM((total, columns), jnp.float32),
            pltpu.VMEM((3, count, columns), jnp.float32),
            pltpu.SemaphoreType.DMA((count,)),
            pltpu.SemaphoreType.DMA,
            pltpu.SemaphoreType.DMA,
        ],
        compiler_params=pltpu.CompilerParams(vmem_limit_bytes=56 << 20),
        name="step",
    )(parity.reshape(1).astype(jnp.int32), weights, recv)

    swap = [(s, s ^ 1) for s in range(stores)]
    kept = halves[0] + lax.ppermute(halves[1], "store", swap)
    chips = stores // 2 * count
    groups = [
        [s * count + b for s in range(c, stores, 2) for b in range(count)] for c in range(2)
    ]
    axes = ("store", "batch")
    pieces = lax.all_to_all(
        kept.reshape(chips, columns // chips, columns),
        axes, split_axis=0, concat_axis=0, axis_index_groups=groups, tiled=True,
    )
    piece = jnp.sum(pieces, axis=0).astype(low)
    layer = lax.all_to_all(
        jnp.broadcast_to(piece[None], (chips,) + piece.shape),
        axes, split_axis=0, concat_axis=0, axis_index_groups=groups, tiled=True,
    ).reshape(columns, columns)
    other = lax.ppermute(layer, "store", swap)
    first = parity == 0
    return jnp.stack(
        [jnp.where(first, layer, other), jnp.where(first, other, layer)]
    ).astype(jnp.float32)


def solution(mesh):
    return jax.shard_map(
        local,
        mesh=mesh,
        in_specs=(
            P("store", "batch", None, None),
            P("store", "batch", None, None),
            P("store", "batch", None, None),
            P("store", "batch"),
            P("store", "batch"),
            P("store", "batch", None, None),
            P("store", "batch", None, None),
            P(),
        ),
        out_specs=P(),
        check_vma=False,
    )
```

time: 446 us -> 158 us (0.35); the launches traced: 437 us -> 157 us
  waiting for transfers between devices: 187 us -> 51.4 us
  matrix products: 107 us -> 0 us
  local copies, waits for them, and re-layouts: 65.1 us -> 3.15 us
  Pallas kernels: 0 us -> 46.3 us
  blocking collectives: 0 us -> 40.9 us
  starting transfers between devices: 46 us -> 13.5 us
  other arithmetic: 18.6 us -> 1.83 us
  between operations: 14 us -> 0.06 us
    psum x1 -> x0, waiting for transfers between devices: 155 us -> none  [local(): result = lax.psum(jnp.stack(gradients), ('store', 'batch'))]
    dot_general x24 -> x0, matrix products: 107 us -> none  [the longest x2 22.8 us: local(): jnp.einsum('cs,vcyf->vsyf', link_full, spread, precision=lax.Precision.HI...]
    pallas_call x0 -> x2, Pallas kernels: none -> 46.3 us  [the longest x1 43 us: local(): pl.pallas_call(step_kernel, out_shape=jax.ShapeDtypeStruct((2, columns, c...]
    all_to_all x0 -> x2, blocking collectives: none -> 40.9 us  [the longest x1 25.6 us: local(): lax.all_to_all(kept.reshape(chips, columns // chips, columns), axes, spli...]
    dot_general x4 -> x0, local copies, waits for them, and re-layouts: 38.9 us -> none  [the longest x2 20.7 us: local(): jnp.einsum('cs,vcyf->vsyf', link_full, spread, precision=lax.Precision.HI...]
    all_to_all x6 -> x1, starting transfers between devices: 34.2 us -> 8.42 us  [local(): lax.all_to_all(send, 'batch', split_axis=0, concat_axis=0, tiled=True)]
    all_to_all x6 -> x1, waiting for transfers between devices: 32 us -> 47.6 us  [local(): lax.all_to_all(send, 'batch', split_axis=0, concat_axis=0, tiled=True)]
    convert_element_type x6 -> x1, other arithmetic: 13.5 us -> 1.46 us  [local(): return jnp.stack([jnp.where(first, layer, other), jnp.where(first, other,...]
  transfers between devices with their start and end apart: 7 -> 3, of which waited for: 5 -> 3; matrix products, arithmetic and copies ran while one was open for 9% -> 0% of each run, Pallas kernels for 0% -> 0%
where the time goes in v1:
time: 158 us; the launch traced here: 157 us
  waiting for transfers between devices  51.4 us (33%)
  Pallas kernels  46.3 us (29%)
  blocking collectives  40.9 us (26%)
  starting transfers between devices  13.5 us (9%)
  local copies, waits for them, and re-layouts  3.15 us (2%)
  other arithmetic  1.83 us (1%)
    all_to_all x1, waiting for transfers between devices, local(): lax.all_to_all(send, 'batch', split_axis=0, concat_axis=0, tiled=True)  47.6 us
    pallas_call x1, Pallas kernels, local(): pl.pallas_call(step_kernel, out_shape=jax.ShapeDtypeStruct((2, columns, c...  43 us
    all_to_all x1, blocking collectives, local(): lax.all_to_all(kept.reshape(chips, columns // chips, columns), axes, spli...  25.6 us
    all_to_all x1, blocking collectives, local(): lax.all_to_all(jnp.broadcast_to(piece[None], (chips,) + piece.shape), axe...  15.3 us
    all_to_all x1, starting transfers between devices, local(): lax.all_to_all(send, 'batch', split_axis=0, concat_axis=0, tiled=True)  8.42 us
    pallas_call x1, Pallas kernels, local(): pl.pallas_call(pack_kernel, out_shape=jax.ShapeDtypeStruct((count, body +...  3.3 us
  transfers between devices with their start and end apart: 3, of which 3 were waited for; matrix products, arithmetic and copies ran while one was open for 0% of the time, Pallas kernels for 0%

profile of v1, /device:TPU:1, one launch (start us, length us, event | category | flops | bytes accessed | tf_op | source)
XLA Modules:
  0.0 157.2 jit_solution(4144236309171033861)
XLA Ops:
  0.0 3.3 %pack.1 = bf16[16,784,128]{2,1,0:T(8,128)(2,1)} custom-call(s32[1,8]{1,0:T(1,128)} %assign.1, s32[1,8]{1,0:T(1,128)} %neighbour.1, bf16[1,8,128,512]{3,2,1,0:T(8,128)(2,1)} %features.1, bf16[1,8,128,128]{3,2,1,0:T(8,128)(2,1)} %diag.1, bf16[1,8,128,128]{3,2,1,0:T(8,128)(2,1)} %coupling.1, s32[1,8,2,512]{3,2,1,0:T(2,128)} %feature_drop.1, ...), custom_call_target="tpu_custom_call" | custom-call | tf_op jit(solution)/shard_map/pack/pallas_call | solution.py:235
  3.3 8.4 %all-to-all-start = ((bf16[16,784,128]{2,1,0:T(8,128)(2,1)}), bf16[16,784,128]{2,1,0:T(8,128)(2,1)S(1)}, u32[]{:S(2)}, u32[]{:S(2)}) async-start(bf16[16,784,128]{2,1,0:T(8,128)(2,1)} %pack.1), calls=%async_computation | async-start | bytes 6422528 | tf_op jit(solution)/shard_map/all_to_all | solution.py:243
  11.7 47.6 %all-to-all-done.recv = bf16[16,784,128]{2,1,0:T(8,128)(2,1)S(1)} async-done(((bf16[16,784,128]{2,1,0:T(8,128)(2,1)}), bf16[16,784,128]{2,1,0:T(8,128)(2,1)S(1)}, u32[]{:S(2)}, u32[]{:S(2)}) %all-to-all-start) | async-done | bytes 3211296 | tf_op jit(solution)/shard_map/all_to_all | solution.py:243
  59.3 0.0 copy-start
  59.3 1.7 %copy-done = bf16[16,784,128]{2,1,0:T(8,128)(2,1)} copy-done((bf16[16,784,128]{2,1,0:T(8,128)(2,1)}, bf16[16,784,128]{2,1,0:T(8,128)(2,1)S(1)}, u32[]{:S(2)}) %copy-start) | copy-done | bytes 3211288
  61.0 43.0 %step.1 = f32[2,512,512]{2,1,0:T(8,128)} custom-call(s32[1]{0:T(128)} %bitcast.core, bf16[2,512,512]{2,1,0:T(8,128)(2,1)} %weights.1, bf16[16,784,128]{2,1,0:T(8,128)(2,1)} %copy-done), custom_call_target="tpu_custom_call" | custom-call | tf_op jit(solution)/shard_map/step/pallas_call | solution.py:246
  104.0 0.0 copy-start.1
  104.1 1.4 slice_bitcast_fusion
  105.5 1.9 %collective-permute-start = (f32[512,512]{1,0:T(8,128)S(1)}, f32[512,512]{1,0:T(8,128)S(1)}, u32[]{:S(2)}, u32[]{:S(2)}) collective-permute-start(f32[512,512]{1,0:T(8,128)S(1)} %slice_bitcast_fusion), channel_id=1, source_target_pairs={{0,16},{16,0},{32,48},{48,32},{64,80},{80,64},{96,112},{112,96},{1... | collective-permute-start | bytes 3145736 | tf_op jit(solution)/shard_map/ppermute | solution.py:273
  107.4 2.3 %collective-permute-done = f32[512,512]{1,0:T(8,128)S(1)} collective-permute-done((f32[512,512]{1,0:T(8,128)S(1)}, f32[512,512]{1,0:T(8,128)S(1)}, u32[]{:S(2)}, u32[]{:S(2)}) %collective-permute-start) | collective-permute-done | bytes 1048608 | tf_op jit(solution)/shard_map/ppermute | solution.py:273
  109.7 0.0 copy-done.1
  109.7 0.2 fusion.1
  109.9 25.6 %all_to_all.15 = f32[64,8,512]{2,1,0:T(8,128)S(1)} all-to-all(f32[64,8,512]{2,1,0:T(8,128)S(1)} %fusion.1), channel_id=1, replica_groups={{0,1,2,3,4,5,6,7,8,9,10,11,12,13,14,15,32,33,34,35,36,37,38,39,40,41,42..., dimensions={0} | all-to-all | bytes 2097152 | tf_op jit(solution)/shard_map/all_to_all | solution.py:279
  135.5 0.1 reduce_sum.9
  135.6 15.3 %all_to_all.16 = bf16[64,8,512]{2,1,0:T(8,128)(2,1)S(1)} all-to-all(bf16[64,8,512]{2,1,0:T(8,128)(2,1)S(1)} %broadcast_in_dim.2), channel_id=1, replica_groups={{0,1,2,3,4,5,6,7,8,9,10,11,12,13,14,15,32,33,34,35,36,37,38,39,40,41,42..., dimensions={0} | all-to-all | bytes 1048576 | tf_op jit(solution)/shard_map/all_to_all | solution.py:284
  151.0 3.2 %collective-permute-start.1 = (bf16[512,512]{1,0:T(8,128)(2,1)S(1)}, bf16[512,512]{1,0:T(8,128)(2,1)S(1)}, u32[]{:S(2)}, u32[]{:S(2)}) collective-permute-start(bf16[512,512]{1,0:T(8,128)(2,1)S(1)} %bitcast.18), channel_id=1, source_target_pairs={{0,16},{16,0},{32,48},{48,32},{64,80},{80,64},{96,112},{112,96},{1... | collective-permute-start | bytes 1572872 | tf_op jit(solution)/shard_map/ppermute | solution.py:288
  154.1 1.5 collective-permute-done.1
  155.7 0.1 select_bitcast_fusion.1
  155.7 1.5 maximum_convert_fusion
  (1 shorter events, 0.0 us)
Async XLA Ops:
  3.3 56.0 %all-to-all-start = ((bf16[16,784,128]{2,1,0:T(8,128)(2,1)}), bf16[16,784,128]{2,1,0:T(8,128)(2,1)S(1)}, u32[]{:S(2)}, u32[]{:S(2)}) async-start(bf16[16,784,128]{2,1,0:T(8,128)(2,1)} %pack.1), calls=%async_computation | async-start | bytes 6422528 | tf_op jit(solution)/shard_map/all_to_all | solution.py:243
  59.3 1.7 %copy-start = (bf16[16,784,128]{2,1,0:T(8,128)(2,1)}, bf16[16,784,128]{2,1,0:T(8,128)(2,1)S(1)}, u32[]{:S(2)}) copy-start(bf16[16,784,128]{2,1,0:T(8,128)(2,1)S(1)} %all-to-all-done.recv) | copy-start | bytes 9633796
  104.0 5.7 %copy-start.1 = (f32[2,512,512]{2,1,0:T(8,128)S(1)}, f32[2,512,512]{2,1,0:T(8,128)}, u32[]{:S(2)}) copy-start(f32[2,512,512]{2,1,0:T(8,128)} %step.1) | copy-start | bytes 6291460
  105.5 4.2 %collective-permute-start = (f32[512,512]{1,0:T(8,128)S(1)}, f32[512,512]{1,0:T(8,128)S(1)}, u32[]{:S(2)}, u32[]{:S(2)}) collective-permute-start(f32[512,512]{1,0:T(8,128)S(1)} %slice_bitcast_fusion), channel_id=1, source_target_pairs={{0,16},{16,0},{32,48},{48,32},{64,80},{80,64},{96,112},{112,96},{1... | collective-permute-start | bytes 3145736 | tf_op jit(solution)/shard_map/ppermute | solution.py:273
  151.0 4.7 %collective-permute-start.1 = (bf16[512,512]{1,0:T(8,128)(2,1)S(1)}, bf16[512,512]{1,0:T(8,128)(2,1)S(1)}, u32[]{:S(2)}, u32[]{:S(2)}) collective-permute-start(bf16[512,512]{1,0:T(8,128)(2,1)S(1)} %bitcast.18), channel_id=1, source_target_pairs={{0,16},{16,0},{32,48},{48,32},{64,80},{80,64},{96,112},{112,96},{1... | collective-permute-start | bytes 1572872 | tf_op jit(solution)/shard_map/ppermute | solution.py:288

commit v2 on v1

--- a/solution.py
+++ b/solution.py
@@ -42,9 +42,8 @@
 
 
 def step_kernel(
-    core, weights, recv, out,
-    rbuf, meta, slots, slot_ids, h0, p0, p1, h1, adj, active, acc, pooled,
-    sems, meta_sem, slot_sem,
+    core, weights, recv, kept, given,
+    slots, slot_ids, h0, p0, p1, h1, adj, active, acc, pooled, slot_sem,
 ):
     count = recv.shape[0]
     columns = weights.shape[1]
@@ -54,12 +53,7 @@
     rows = 2 * nodes
     low = jnp.bfloat16
 
-    meta_copy = pltpu.make_async_copy(recv.at[:, pl.ds(body, META), :], meta, meta_sem)
-    meta_copy.start()
-    for s in range(count):
-        pltpu.make_async_copy(recv.at[s, pl.ds(0, body), :], rbuf.at[s], sems.at[s]).start()
-    meta_copy.wait()
-    slots[...] = meta[...].astype(jnp.float32)
+    slots[...] = recv[:, pl.ds(body, META), :].astype(jnp.float32)
     pooled[2, :, pl.ds(0, LANES)] = slots[:, 2 * blocks + 2, :]
     nbr = slots[:, 2 * blocks + 2, :].astype(jnp.int32) - 1
     own = lax.broadcasted_iota(jnp.int32, nbr.shape, 0)
@@ -74,11 +68,10 @@
     pl.run_scoped(put_ids, pltpu.VMEM((count, LANES), jnp.int32))
 
     def project(s, carry):
-        pltpu.make_async_copy(recv.at[s, pl.ds(0, body), :], rbuf.at[s], sems.at[s]).wait()
         n = slot_ids[s, 0]
-        own_rows = rbuf[s, pl.ds(0, blocks * nodes), :].reshape(blocks, nodes, LANES)
-        diag = rbuf[s, pl.ds(blocks * nodes, nodes), :]
-        coupling = rbuf[s, pl.ds((blocks + 1) * nodes, nodes), :]
+        own_rows = recv[s, pl.ds(0, blocks * nodes), :].reshape(blocks, nodes, LANES)
+        diag = recv[s, pl.ds(blocks * nodes, nodes), :]
+        coupling = recv[s, pl.ds((blocks + 1) * nodes, nodes), :]
         zero = jnp.zeros((), low)
         for v in range(2):
             pieces = []
@@ -186,17 +179,25 @@
 
     lax.fori_loop(0, count, second_back, 0)
 
-    keep_one = core[0] ^ 1
-    keep_zero = core[0]
     chunk = 4 * rows
-    out[...] = jnp.zeros_like(out)
+    kept[...] = jnp.zeros_like(kept)
+    given[...] = jnp.zeros_like(given)
+
+    def add(layer, part):
+        @pl.when(core[0] == layer)
+        def _():
+            kept[...] = kept[...] + part
+
+        @pl.when(core[0] != layer)
+        def _():
+            given[...] = given[...] + part
 
     def second_weights(i, carry):
         span = pl.ds(i * chunk, chunk)
         grad = acc[span, :].astype(low)
         acc[span, :] = jnp.zeros((chunk, columns), jnp.float32)
         hidden = h1[span, :]
-        out[keep_one] = out[keep_one] + dot(hidden, grad, ((0,), (0,)))
+        add(1, dot(hidden, grad, ((0,), (0,))))
         below = dot(grad, weights[1], ((1,), (1,)))
         p0[span, :] = jnp.where(hidden > 0, below, 0.0).astype(low)
         return carry
@@ -212,9 +213,7 @@
 
     def first_weights(i, carry):
         span = pl.ds(i * chunk, chunk)
-        out[keep_zero] = out[keep_zero] + dot(
-            h0[span, :], acc[span, :].astype(low), ((0,), (0,))
-        )
+        add(0, dot(h0[span, :], acc[span, :].astype(low), ((0,), (0,))))
         return carry
 
     lax.fori_loop(0, count // 4, first_weights, 0)
@@ -231,7 +230,6 @@
     low = jnp.bfloat16
     smem = pl.BlockSpec(memory_space=pltpu.SMEM)
     vmem = pl.BlockSpec(memory_space=pltpu.VMEM)
-    raw = pl.BlockSpec(memory_space=pl.ANY)
     send = pl.pallas_call(
         pack_kernel,
         out_shape=jax.ShapeDtypeStruct((count, body + META, LANES), low),
@@ -240,17 +238,17 @@
         scratch_shapes=[pltpu.VMEM((count, META, LANES), jnp.float32)],
         name="pack",
     )(assignment, neighbour, features, diag_blocks, coupling_blocks, feature_drop, edge_drop)
+    parity = lax.axis_index("store") % 2
+    send, parity = lax.optimization_barrier((send, parity))
     recv = lax.all_to_all(send, "batch", split_axis=0, concat_axis=0, tiled=True)
-    parity = lax.axis_index("store") % 2
     total = count * 2 * nodes
-    halves = pl.pallas_call(
+    half = jax.ShapeDtypeStruct((columns, columns), jnp.float32)
+    kept, given = pl.pallas_call(
         step_kernel,
-        out_shape=jax.ShapeDtypeStruct((2, columns, columns), jnp.float32),
-        in_specs=[smem, vmem, raw],
-        out_specs=vmem,
+        out_shape=[half, half],
+        in_specs=[smem, vmem, vmem],
+        out_specs=[vmem, vmem],
         scratch_shapes=[
-            pltpu.VMEM((count, body, LANES), low),
-            pltpu.VMEM((count, META, LANES), low),
             pltpu.VMEM((count, META, LANES), jnp.float32),
             pltpu.SMEM((count, LANES), jnp.int32),
             pltpu.VMEM((total, columns), low),
@@ -261,8 +259,6 @@
             pltpu.VMEM((total, columns), low),
             pltpu.VMEM((total, columns), jnp.float32),
             pltpu.VMEM((3, count, columns), jnp.float32),
-            pltpu.SemaphoreType.DMA((count,)),
-            pltpu.SemaphoreType.DMA,
             pltpu.SemaphoreType.DMA,
         ],
         compiler_params=pltpu.CompilerParams(vmem_limit_bytes=56 << 20),
@@ -270,7 +266,7 @@
     )(parity.reshape(1).astype(jnp.int32), weights, recv)
 
     swap = [(s, s ^ 1) for s in range(stores)]
-    kept = halves[0] + lax.ppermute(halves[1], "store", swap)
+    kept = kept + lax.ppermute(given, "store", swap)
     chips = stores // 2 * count
     groups = [
         [s * count + b for s in range(c, stores, 2) for b in range(count)] for c in range(2)

time: 158 us -> 147 us (0.930)
  waiting for transfers between devices: 51.4 us -> 4.03 us
  blocking collectives: 40.9 us -> 87.7 us
  starting transfers between devices: 13.5 us -> 5.21 us
  local copies, waits for them, and re-layouts: 3.15 us -> 0.04 us
    all_to_all x0 -> x1, blocking collectives: none -> 47.9 us  [local(): lax.all_to_all(send, 'batch', split_axis=0, concat_axis=0, tiled=True)]
    all_to_all x1 -> x0, waiting for transfers between devices: 47.6 us -> none  [local(): lax.all_to_all(send, 'batch', split_axis=0, concat_axis=0, tiled=True)]
    all_to_all x1 -> x0, starting transfers between devices: 8.42 us -> none  [local(): lax.all_to_all(send, 'batch', split_axis=0, concat_axis=0, tiled=True)]
    unnamed x4 -> x0, local copies, waits for them, and re-layouts: 1.67 us -> none
  transfers between devices with their start and end apart: 3 -> 2, of which waited for: 3 -> 2; matrix products, arithmetic and copies ran while one was open for 0% -> 0% of each run, Pallas kernels for 0% -> 0%
where the time goes in v2:
time: 147 us
  blocking collectives  87.7 us (60%)
  Pallas kernels  47.1 us (32%)
  starting transfers between devices  5.21 us (4%)
  waiting for transfers between devices  4.03 us (3%)
  other arithmetic  3.06 us (2%)
    all_to_all x1, blocking collectives, local(): lax.all_to_all(send, 'batch', split_axis=0, concat_axis=0, tiled=True)  47.9 us
    pallas_call x1, Pallas kernels, local(): pl.pallas_call(step_kernel, out_shape=[half, half], in_specs=[smem, vmem,...  43.8 us
    all_to_all x1, blocking collectives, local(): lax.all_to_all(kept.reshape(chips, columns // chips, columns), axes, spli...  24.5 us
    all_to_all x1, blocking collectives, local(): lax.all_to_all(jnp.broadcast_to(piece[None], (chips,) + piece.shape), axe...  15.3 us
    pallas_call x1, Pallas kernels, local(): pl.pallas_call(pack_kernel, out_shape=jax.ShapeDtypeStruct((count, body +...  3.35 us
    ppermute x1, starting transfers between devices, local(): other = lax.ppermute(layer, 'store', swap)  3.15 us
  transfers between devices with their start and end apart: 2, of which 2 were waited for; matrix products, arithmetic and copies ran while one was open for 0% of the time, Pallas kernels for 0%

profile of v2, /device:TPU:1, one launch (start us, length us, event | category | flops | bytes accessed | tf_op | source)
XLA Modules:
  0.0 147.2 jit_solution(5269027794159509553)
XLA Ops:
  0.0 3.3 %pack.1 = bf16[16,784,128]{2,1,0:T(8,128)(2,1)} custom-call(s32[1,8]{1,0:T(1,128)} %assign.1, s32[1,8]{1,0:T(1,128)} %neighbour.1, bf16[1,8,128,512]{3,2,1,0:T(8,128)(2,1)} %features.1, bf16[1,8,128,128]{3,2,1,0:T(8,128)(2,1)} %diag.1, bf16[1,8,128,128]{3,2,1,0:T(8,128)(2,1)} %coupling.1, s32[1,8,2,512]{3,2,1,0:T(2,128)} %feature_drop.1, ...), custom_call_target="tpu_custom_call" | custom-call | tf_op jit(solution)/shard_map/pack/pallas_call | solution.py:233
  3.3 47.9 %all_to_all.15.recv = bf16[16,784,128]{2,1,0:T(8,128)(2,1)} all-to-all(bf16[16,784,128]{2,1,0:T(8,128)(2,1)} %pack.1), channel_id=1, replica_groups=mesh['store'=8,'batch'=16] {'batch'}, dimensions={0} | all-to-all | bytes 6422528 | tf_op jit(solution)/shard_map/all_to_all | solution.py:243
  51.2 43.8 %step.1 = (f32[512,512]{1,0:T(8,128)}, f32[512,512]{1,0:T(8,128)}) custom-call(s32[1]{0:T(128)} %bitcast.core, bf16[2,512,512]{2,1,0:T(8,128)(2,1)} %weights.1, bf16[16,784,128]{2,1,0:T(8,128)(2,1)} %all_to_all.15.recv), custom_call_target="tpu_custom_call" | custom-call | tf_op jit(solution)/shard_map/step/pallas_call | solution.py:246
  95.0 2.1 %collective-permute-start = (f32[512,512]{1,0:T(8,128)}, f32[512,512]{1,0:T(8,128)S(1)}, u32[]{:S(2)}, u32[]{:S(2)}) collective-permute-start(f32[512,512]{1,0:T(8,128)} %get-tuple-element.12), channel_id=1, source_target_pairs={{0,16},{16,0},{32,48},{48,32},{64,80},{80,64},{96,112},{112,96},{1... | collective-permute-start | bytes 3145736 | tf_op jit(solution)/shard_map/ppermute | solution.py:269
  97.1 2.5 %collective-permute-done = f32[512,512]{1,0:T(8,128)S(1)} collective-permute-done((f32[512,512]{1,0:T(8,128)}, f32[512,512]{1,0:T(8,128)S(1)}, u32[]{:S(2)}, u32[]{:S(2)}) %collective-permute-start) | collective-permute-done | bytes 1048608 | tf_op jit(solution)/shard_map/ppermute | solution.py:269
  99.6 1.4 add_bitcast_fusion
  101.0 24.5 %all_to_all.16 = f32[64,8,512]{2,1,0:T(8,128)S(1)} all-to-all(f32[64,8,512]{2,1,0:T(8,128)S(1)} %add_bitcast_fusion), channel_id=1, replica_groups={{0,1,2,3,4,5,6,7,8,9,10,11,12,13,14,15,32,33,34,35,36,37,38,39,40,41,42..., dimensions={0} | all-to-all | bytes 2097152 | tf_op jit(solution)/shard_map/all_to_all | solution.py:275
  125.5 0.1 reduce_sum.9
  125.6 15.3 %all_to_all.17 = bf16[64,8,512]{2,1,0:T(8,128)(2,1)S(1)} all-to-all(bf16[64,8,512]{2,1,0:T(8,128)(2,1)S(1)} %broadcast_in_dim.2), channel_id=1, replica_groups={{0,1,2,3,4,5,6,7,8,9,10,11,12,13,14,15,32,33,34,35,36,37,38,39,40,41,42..., dimensions={0} | all-to-all | bytes 1048576 | tf_op jit(solution)/shard_map/all_to_all | solution.py:280
  141.0 3.2 %collective-permute-start.1 = (bf16[512,512]{1,0:T(8,128)(2,1)S(1)}, bf16[512,512]{1,0:T(8,128)(2,1)S(1)}, u32[]{:S(2)}, u32[]{:S(2)}) collective-permute-start(bf16[512,512]{1,0:T(8,128)(2,1)S(1)} %bitcast.10), channel_id=1, source_target_pairs={{0,16},{16,0},{32,48},{48,32},{64,80},{80,64},{96,112},{112,96},{1... | collective-permute-start | bytes 1572872 | tf_op jit(solution)/shard_map/ppermute | solution.py:284
  144.1 1.5 %collective-permute-done.1 = bf16[512,512]{1,0:T(8,128)(2,1)S(1)} collective-permute-done((bf16[512,512]{1,0:T(8,128)(2,1)S(1)}, bf16[512,512]{1,0:T(8,128)(2,1)S(1)}, u32[]{:S(2)}, u32[]{:S(2)}) %collective-permute-start.1) | collective-permute-done | bytes 524320 | tf_op jit(solution)/shard_map/ppermute | solution.py:284
  145.6 0.1 select_bitcast_fusion.1
  145.7 1.5 maximum_convert_fusion
  (1 shorter events, 0.0 us)
Async XLA Ops:
  95.0 4.6 %collective-permute-start = (f32[512,512]{1,0:T(8,128)}, f32[512,512]{1,0:T(8,128)S(1)}, u32[]{:S(2)}, u32[]{:S(2)}) collective-permute-start(f32[512,512]{1,0:T(8,128)} %get-tuple-element.12), channel_id=1, source_target_pairs={{0,16},{16,0},{32,48},{48,32},{64,80},{80,64},{96,112},{112,96},{1... | collective-permute-start | bytes 3145736 | tf_op jit(solution)/shard_map/ppermute | solution.py:269
  141.0 4.7 %collective-permute-start.1 = (bf16[512,512]{1,0:T(8,128)(2,1)S(1)}, bf16[512,512]{1,0:T(8,128)(2,1)S(1)}, u32[]{:S(2)}, u32[]{:S(2)}) collective-permute-start(bf16[512,512]{1,0:T(8,128)(2,1)S(1)} %bitcast.10), channel_id=1, source_target_pairs={{0,16},{16,0},{32,48},{48,32},{64,80},{80,64},{96,112},{112,96},{1... | collective-permute-start | bytes 1572872 | tf_op jit(solution)/shard_map/ppermute | solution.py:284

commit v3 on v2

v3 whole, which is shorter than its diff:
```python
import jax
import jax.numpy as jnp
from jax import lax
from jax.experimental import pallas as pl
from jax.experimental.pallas import tpu as pltpu
from jax.sharding import PartitionSpec as P

SOFTMAX_TEMPER = 0.5
EPSILON = 1e-05

LANES = 128
META = 16
UA = 8
UB = 16
UC = 16
CHUNK = 16


def pack_kernel(
    assign, neighbour, features, diag, coupling, feature_drop, edge_drop, send, meta
):
    owned, nodes, columns = features.shape[1:]
    blocks = columns // LANES
    meta[...] = jnp.zeros_like(meta)
    send[:, pl.ds(0, (blocks + 2) * nodes), :] = jnp.zeros(
        (send.shape[0], (blocks + 2) * nodes, LANES), jnp.bfloat16
    )
    for k in range(owned):
        target = assign[0, k]
        for j in range(blocks):
            send[target, pl.ds(j * nodes, nodes), :] = features[0, k, :, pl.ds(j * LANES, LANES)]
        send[target, pl.ds(blocks * nodes, nodes), :] = diag[0, k]
        send[target, pl.ds((blocks + 1) * nodes, nodes), :] = coupling[0, k]
        for v in range(2):
            for j in range(blocks):
                meta[target, v * blocks + j, :] = feature_drop[
                    0, k, v, pl.ds(j * LANES, LANES)
                ].astype(jnp.float32)
            meta[target, 2 * blocks + v, :] = edge_drop[0, k, v, :].astype(jnp.float32)
        slot = neighbour[0, k] // owned + 1
        meta[target, 2 * blocks + 2, :] = jnp.full((LANES,), slot, jnp.float32)
    send[:, pl.ds((blocks + 2) * nodes, META), :] = meta[...].astype(jnp.bfloat16)


def dot(a, b, contract, precision=None):
    return lax.dot_general(
        a, b, (contract, ((), ())), precision=precision, preferred_element_type=jnp.float32
    )


def step_kernel(
    core, weights, recv, kept, given,
    slots, links, first, extra_count, extra_to, extra_from,
    h0, p0, p1, h1, near, far, active, sums, pooled, link_sem,
):
    count = recv.shape[0]
    columns = weights.shape[1]
    blocks = columns // LANES
    nodes = near.shape[1]
    body = (blocks + 2) * nodes
    rows = 2 * nodes
    chunk = sums.shape[0] // rows
    low = jnp.bfloat16

    slots[...] = recv[:, pl.ds(body, META), :].astype(jnp.float32)
    pooled[2, :, pl.ds(0, LANES)] = slots[:, 2 * blocks + 2, :]
    found = slots[:, 2 * blocks + 2, :].astype(jnp.int32) - 1
    itself = lax.broadcasted_iota(jnp.int32, found.shape, 0)

    def put_links(staged):
        staged[...] = jnp.where(found < 0, itself, found)
        copy = pltpu.make_async_copy(staged, links, link_sem)
        copy.start()
        copy.wait()

    pl.run_scoped(put_links, pltpu.VMEM((count, LANES), jnp.int32))

    for s in range(count):
        first[s] = count
    for i in range(count // chunk):
        extra_count[i] = 0

    def enlist(s, carry):
        n = links[s, 0]
        i = n // chunk
        taken = first[n] != count

        @pl.when(taken)
        def _():
            k = extra_count[i]
            extra_to[i * count + k] = n
            extra_from[i * count + k] = s
            extra_count[i] = k + 1

        @pl.when(jnp.logical_not(taken))
        def _():
            first[n] = s

        return carry

    lax.fori_loop(0, count, enlist, 0)
    far[pl.ds(2 * count, 2)] = jnp.zeros((2, nodes, nodes), low)

    def each(width, stage, then=None):
        def steps(i, carry):
            for u in range(width):
                stage(i * width + u)
            if then is not None:
                then(pl.ds(i * width * rows, width * rows))
            return carry

        lax.fori_loop(0, count // width, steps, 0)

    def part(s, v):
        return pl.ds(s * rows + v * nodes, nodes)

    def project(s):
        n = links[s, 0]
        for v in range(2):
            pieces = []
            for j in range(blocks):
                keep = slots[s, pl.ds(v * blocks + j, 1), :].astype(low)
                pieces.append(recv[s, pl.ds(j * nodes, nodes), :] * keep)
            h0[part(s, v), :] = jnp.concatenate(pieces, axis=1)
            own_keep = slots[s, pl.ds(2 * blocks + v, 1), :].astype(low)
            far_keep = slots[n, pl.ds(2 * blocks + v, 1), :].astype(low)
            near[2 * s + v] = recv[s, pl.ds(blocks * nodes, nodes), :] * own_keep
            far[2 * s + v] = recv[s, pl.ds((blocks + 1) * nodes, nodes), :] * far_keep

    def project_rows(span):
        p0[span, :] = dot(h0[span, :], weights[0], ((1,), (0,))).astype(low)

    each(UA, project, project_rows)

    def gather(source, s, v):
        n = links[s, 0]
        return dot(
            jnp.concatenate([near[2 * s + v], far[2 * s + v]], axis=1),
            jnp.concatenate([source[part(s, v), :], source[part(n, v), :]], axis=0),
            ((1,), (0,)),
        )

    def first_layer(s):
        for v in range(2):
            h1[part(s, v), :] = jnp.maximum(gather(p0, s, v), 0.0).astype(low)

    def first_rows(span):
        p1[span, :] = dot(h1[span, :], weights[1], ((1,), (0,))).astype(low)

    each(UB, first_layer, first_rows)

    def second_layer(s):
        for v in range(2):
            summed = jnp.maximum(gather(p1, s, v), 0.0)
            active[part(s, v), :] = jnp.where(summed > 0, 1.0, 0.0).astype(low)
            pooled[v, pl.ds(s, 1), :] = jnp.sum(summed, axis=0, keepdims=True) * (1.0 / nodes)

    each(UC, second_layer)

    flags = jnp.where(pooled[2, :, pl.ds(0, LANES)] > 0.5, 1.0, 0.0)
    occ_col = flags[:, 0:1]
    occ_row = dot(
        jnp.full((8, LANES), 1.0 / LANES, jnp.float32), flags, ((1,), (1,)), lax.Precision.HIGHEST
    )[0:1, :]
    means = [pooled[0], pooled[1]]
    inv = [lax.rsqrt(jnp.mean(e * e, axis=-1, keepdims=True) + EPSILON) for e in means]
    unit = [e * i for e, i in zip(means, inv)]
    scale = 1.0 / (columns * SOFTMAX_TEMPER)
    high = lax.Precision.HIGHEST
    scores = dot(unit[0], unit[1], ((1,), (1,)), high) * scale
    weighted = jnp.exp(scores) * occ_row
    totals = jnp.where(occ_col > 0.5, jnp.sum(weighted, axis=1, keepdims=True), 1.0)
    row_id = lax.broadcasted_iota(jnp.int32, (count, count), 0)
    col_id = lax.broadcasted_iota(jnp.int32, (count, count), 1)
    eye = jnp.where(row_id == col_id, 1.0, 0.0)
    coeffs = (weighted / totals - eye) * occ_col
    unit_grad = [
        dot(coeffs, unit[1], ((1,), (0,)), high) * scale,
        dot(coeffs, unit[0], ((0,), (0,)), high) * scale,
    ]
    for v in range(2):
        grad = (
            inv[v] * unit_grad[v]
            - (inv[v] ** 3 * jnp.sum(means[v] * unit_grad[v], axis=-1, keepdims=True) / columns)
            * means[v]
        )
        pooled[v] = (grad / nodes).astype(low).astype(jnp.float32)

    def add(layer, part_sum):
        @pl.when(core[0] == layer)
        def _():
            kept[...] = kept[...] + part_sum

        @pl.when(core[0] != layer)
        def _():
            given[...] = given[...] + part_sum

    kept[...] = jnp.zeros_like(kept)
    given[...] = jnp.zeros_like(given)

    def spread(i, grad_of):
        for u in range(chunk):
            s = i * chunk + u
            a = first[s]
            b = jnp.minimum(a, count - 1)
            for v in range(2):
                sums[pl.ds(u * rows + v * nodes, nodes), :] = dot(
                    jnp.concatenate([near[2 * s + v], far[2 * a + v]], axis=0),
                    jnp.concatenate([grad_of(s, v), grad_of(b, v)], axis=0),
                    ((0,), (0,)),
                )

        def further(k, carry):
            a = extra_from[i * count + k]
            u = extra_to[i * count + k] - i * chunk
            for v in range(2):
                mine = part(u, v)
                sums[mine, :] = sums[mine, :] + dot(far[2 * a + v], grad_of(a, v), ((0,), (0,)))
            return carry

        lax.fori_loop(0, extra_count[i], further, 0)
        return sums[...].astype(low)

    def second_grad(s, v):
        return active[part(s, v), :] * pooled[v, pl.ds(s, 1), :].astype(low)

    def second_back(i, carry):
        grad = spread(i, second_grad)
        span = pl.ds(i * chunk * rows, chunk * rows)
        hidden = h1[span, :]
        add(1, dot(hidden, grad, ((0,), (0,))))
        below = dot(grad, weights[1], ((1,), (1,)))
        p0[span, :] = jnp.where(hidden > 0, below, 0.0).astype(low)
        return carry

    lax.fori_loop(0, count // chunk, second_back, 0)

    def first_grad(s, v):
        return p0[part(s, v), :]

    def first_back(i, carry):
        grad = spread(i, first_grad)
        add(0, dot(h0[pl.ds(i * chunk * rows, chunk * rows), :], grad, ((0,), (0,))))
        return carry

    lax.fori_loop(0, count // chunk, first_back, 0)


def local(
    features, diag_blocks, coupling_blocks, neighbour, assignment, feature_drop, edge_drop, weights
):
    count = lax.axis_size("batch")
    stores = lax.axis_size("store")
    _, owned, nodes, columns = features.shape
    blocks = columns // LANES
    body = (blocks + 2) * nodes
    low = jnp.bfloat16
    smem = pl.BlockSpec(memory_space=pltpu.SMEM)
    vmem = pl.BlockSpec(memory_space=pltpu.VMEM)
    send = pl.pallas_call(
        pack_kernel,
        out_shape=jax.ShapeDtypeStruct((count, body + META, LANES), low),
        in_specs=[smem, smem, vmem, vmem, vmem, vmem, vmem],
        out_specs=vmem,
        scratch_shapes=[pltpu.VMEM((count, META, LANES), jnp.float32)],
        name="pack",
    )(assignment, neighbour, features, diag_blocks, coupling_blocks, feature_drop, edge_drop)
    parity = lax.axis_index("store") % 2
    send, parity = lax.optimization_barrier((send, parity))
    recv = lax.all_to_all(send, "batch", split_axis=0, concat_axis=0, tiled=True)
    total = count * 2 * nodes
    half = jax.ShapeDtypeStruct((columns, columns), jnp.float32)
    kept, given = pl.pallas_call(
        step_kernel,
        out_shape=[half, half],
        in_specs=[smem, vmem, vmem],
        out_specs=[vmem, vmem],
        scratch_shapes=[
            pltpu.VMEM((count, META, LANES), jnp.float32),
            pltpu.SMEM((count, LANES), jnp.int32),
            pltpu.SMEM((count,), jnp.int32),
            pltpu.SMEM((count,), jnp.int32),
            pltpu.SMEM((count * count,), jnp.int32),
            pltpu.SMEM((count * count,), jnp.int32),
            pltpu.VMEM((total, columns), low),
            pltpu.VMEM((total, columns), low),
            pltpu.VMEM((total, columns), low),
            pltpu.VMEM((total, columns), low),
            pltpu.VMEM((2 * count, nodes, nodes), low),
            pltpu.VMEM((2 * count + 2, nodes, nodes), low),
            pltpu.VMEM((total, columns), low),
            pltpu.VMEM((CHUNK * 2 * nodes, columns), jnp.float32),
            pltpu.VMEM((3, count, columns), jnp.float32),
            pltpu.SemaphoreType.DMA,
        ],
        compiler_params=pltpu.CompilerParams(vmem_limit_bytes=56 << 20),
        name="step",
    )(parity.reshape(1).astype(jnp.int32), weights, recv)

    swap = [(s, s ^ 1) for s in range(stores)]
    kept = kept + lax.ppermute(given, "store", swap)
    chips = stores // 2 * count
    groups = [
        [s * count + b for s in range(c, stores, 2) for b in range(count)] for c in range(2)
    ]
    axes = ("store", "batch")
    pieces = lax.all_to_all(
        kept.reshape(chips, columns // chips, columns),
        axes, split_axis=0, concat_axis=0, axis_index_groups=groups, tiled=True,
    )
    piece = jnp.sum(pieces, axis=0).astype(low)
    layer = lax.all_to_all(
        jnp.broadcast_to(piece[None], (chips,) + piece.shape),
        axes, split_axis=0, concat_axis=0, axis_index_groups=groups, tiled=True,
    ).reshape(columns, columns)
    other = lax.ppermute(layer, "store", swap)
    first = parity == 0
    return jnp.stack(
        [jnp.where(first, layer, other), jnp.where(first, other, layer)]
    ).astype(jnp.float32)


def solution(mesh):
    return jax.shard_map(
        local,
        mesh=mesh,
        in_specs=(
            P("store", "batch", None, None),
            P("store", "batch", None, None),
            P("store", "batch", None, None),
            P("store", "batch"),
            P("store", "batch"),
            P("store", "batch", None, None),
            P("store", "batch", None, None),
            P(),
        ),
        out_specs=P(),
        check_vma=False,
    )
```

time: 147 us -> 132 us (0.90); the launches traced: 147 us -> 131 us
  Pallas kernels: 47.1 us -> 30 us
  blocking collectives: 87.7 us -> 89.4 us
    pallas_call x1, Pallas kernels: 43.8 us -> 26.2 us  [local(): pl.pallas_call(step_kernel, out_shape=[half, half], in_specs=[smem, vmem,...]
    all_to_all x1, blocking collectives: 24.5 us -> 26.2 us  [local(): lax.all_to_all(kept.reshape(chips, columns // chips, columns), axes, spli...]
where the time goes in v3:
time: 132 us; the launch traced here: 131 us
  blocking collectives  89.4 us (68%)
  Pallas kernels  30 us (23%)
  starting transfers between devices  4.17 us (3%)
  waiting for transfers between devices  4.03 us (3%)
  other arithmetic  3.06 us (2%)
    all_to_all x1, blocking collectives, local(): lax.all_to_all(send, 'batch', split_axis=0, concat_axis=0, tiled=True)  47.9 us
    pallas_call x1, Pallas kernels, local(): pl.pallas_call(step_kernel, out_shape=[half, half], in_specs=[smem, vmem,...  26.2 us
    all_to_all x1, blocking collectives, local(): lax.all_to_all(kept.reshape(chips, columns // chips, columns), axes, spli...  26.2 us
    all_to_all x1, blocking collectives, local(): lax.all_to_all(jnp.broadcast_to(piece[None], (chips,) + piece.shape), axe...  15.3 us
    pallas_call x1, Pallas kernels, local(): pl.pallas_call(pack_kernel, out_shape=jax.ShapeDtypeStruct((count, body +...  3.73 us
    ppermute x1, starting transfers between devices, local(): other = lax.ppermute(layer, 'store', swap)  3.15 us
  transfers between devices with their start and end apart: 2, of which 2 were waited for; matrix products, arithmetic and copies ran while one was open for 0% of the time, Pallas kernels for 0%

profile of v3, /device:TPU:1, one launch (start us, length us, event | category | flops | bytes accessed | tf_op | source)
XLA Modules:
  0.0 130.7 jit_solution(4965391383483240043)
XLA Ops:
  0.0 3.7 %pack.1 = bf16[16,784,128]{2,1,0:T(8,128)(2,1)} custom-call(s32[1,8]{1,0:T(1,128)} %assign.1, s32[1,8]{1,0:T(1,128)} %neighbour.1, bf16[1,8,128,512]{3,2,1,0:T(8,128)(2,1)} %features.1, bf16[1,8,128,128]{3,2,1,0:T(8,128)(2,1)} %diag.1, bf16[1,8,128,128]{3,2,1,0:T(8,128)(2,1)} %coupling.1, s32[1,8,2,512]{3,2,1,0:T(2,128)} %feature_drop.1, ...), custom_call_target="tpu_custom_call" | custom-call | tf_op jit(solution)/shard_map/pack/pallas_call | solution.py:260
  3.7 47.9 %all_to_all.15.recv = bf16[16,784,128]{2,1,0:T(8,128)(2,1)} all-to-all(bf16[16,784,128]{2,1,0:T(8,128)(2,1)} %pack.1), channel_id=1, replica_groups=mesh['store'=8,'batch'=16] {'batch'}, dimensions={0} | all-to-all | bytes 6422528 | tf_op jit(solution)/shard_map/all_to_all | solution.py:270
  51.6 26.2 %step.1 = (f32[512,512]{1,0:T(8,128)}, f32[512,512]{1,0:T(8,128)}) custom-call(s32[1]{0:T(128)} %bitcast.core, bf16[2,512,512]{2,1,0:T(8,128)(2,1)} %weights.1, bf16[16,784,128]{2,1,0:T(8,128)(2,1)} %all_to_all.15.recv), custom_call_target="tpu_custom_call" | custom-call | tf_op jit(solution)/shard_map/step/pallas_call | solution.py:273
  77.9 1.0 collective-permute-start
  78.9 2.5 %collective-permute-done = f32[512,512]{1,0:T(8,128)S(1)} collective-permute-done((f32[512,512]{1,0:T(8,128)}, f32[512,512]{1,0:T(8,128)S(1)}, u32[]{:S(2)}, u32[]{:S(2)}) %collective-permute-start) | collective-permute-done | bytes 1048608 | tf_op jit(solution)/shard_map/ppermute | solution.py:301
  81.4 1.4 %add_bitcast_fusion = f32[64,8,512]{2,1,0:T(8,128)S(1)} fusion(f32[512,512]{1,0:T(8,128)} %get-tuple-element.11, f32[512,512]{1,0:T(8,128)S(1)} %collective-permute-done), kind=kLoop, calls=%fused_computation.1 | loop fusion | flops 262144 | bytes 3145728 | tf_op jit(solution)/shard_map/reshape | solution.py:308
  82.8 26.2 %all_to_all.16 = f32[64,8,512]{2,1,0:T(8,128)S(1)} all-to-all(f32[64,8,512]{2,1,0:T(8,128)S(1)} %add_bitcast_fusion), channel_id=1, replica_groups={{0,1,2,3,4,5,6,7,8,9,10,11,12,13,14,15,32,33,34,35,36,37,38,39,40,41,42..., dimensions={0} | all-to-all | bytes 2097152 | tf_op jit(solution)/shard_map/all_to_all | solution.py:307
  109.0 0.1 reduce_sum.9
  109.1 15.3 %all_to_all.17 = bf16[64,8,512]{2,1,0:T(8,128)(2,1)S(1)} all-to-all(bf16[64,8,512]{2,1,0:T(8,128)(2,1)S(1)} %broadcast_in_dim.2), channel_id=1, replica_groups={{0,1,2,3,4,5,6,7,8,9,10,11,12,13,14,15,32,33,34,35,36,37,38,39,40,41,42..., dimensions={0} | all-to-all | bytes 1048576 | tf_op jit(solution)/shard_map/all_to_all | solution.py:312
  124.5 3.2 %collective-permute-start.1 = (bf16[512,512]{1,0:T(8,128)(2,1)S(1)}, bf16[512,512]{1,0:T(8,128)(2,1)S(1)}, u32[]{:S(2)}, u32[]{:S(2)}) collective-permute-start(bf16[512,512]{1,0:T(8,128)(2,1)S(1)} %bitcast.10), channel_id=1, source_target_pairs={{0,16},{16,0},{32,48},{48,32},{64,80},{80,64},{96,112},{112,96},{1... | collective-permute-start | bytes 1572872 | tf_op jit(solution)/shard_map/ppermute | solution.py:316
  127.6 1.5 %collective-permute-done.1 = bf16[512,512]{1,0:T(8,128)(2,1)S(1)} collective-permute-done((bf16[512,512]{1,0:T(8,128)(2,1)S(1)}, bf16[512,512]{1,0:T(8,128)(2,1)S(1)}, u32[]{:S(2)}, u32[]{:S(2)}) %collective-permute-start.1) | collective-permute-done | bytes 524320 | tf_op jit(solution)/shard_map/ppermute | solution.py:316
  129.2 0.1 select_bitcast_fusion.1
  129.2 1.5 %maximum_convert_fusion = f32[2,512,512]{2,1,0:T(8,128)} fusion(bf16[1,512,512]{2,1,0:T(8,128)(2,1)S(1)} %get-tuple-element.14, bf16[1,512,512]{2,1,0:T(8,128)(2,1)S(1)} %get-tuple-element.13), kind=kLoop, calls=%fused_computation | loop fusion | flops 1048576 | bytes 3145728 | tf_op jit(solution)/shard_map/convert_element_type | solution.py:320
  (1 shorter events, 0.0 us)
Async XLA Ops:
  77.9 3.5 %collective-permute-start = (f32[512,512]{1,0:T(8,128)}, f32[512,512]{1,0:T(8,128)S(1)}, u32[]{:S(2)}, u32[]{:S(2)}) collective-permute-start(f32[512,512]{1,0:T(8,128)} %get-tuple-element.12), channel_id=1, source_target_pairs={{0,16},{16,0},{32,48},{48,32},{64,80},{80,64},{96,112},{112,96},{1... | collective-permute-start | bytes 3145736 | tf_op jit(solution)/shard_map/ppermute | solution.py:301
  124.5 4.7 %collective-permute-start.1 = (bf16[512,512]{1,0:T(8,128)(2,1)S(1)}, bf16[512,512]{1,0:T(8,128)(2,1)S(1)}, u32[]{:S(2)}, u32[]{:S(2)}) collective-permute-start(bf16[512,512]{1,0:T(8,128)(2,1)S(1)} %bitcast.10), channel_id=1, source_target_pairs={{0,16},{16,0},{32,48},{48,32},{64,80},{80,64},{96,112},{112,96},{1... | collective-permute-start | bytes 1572872 | tf_op jit(solution)/shard_map/ppermute | solution.py:316

commit v4 on v3

--- a/solution.py
+++ b/solution.py
@@ -263,6 +263,7 @@
         in_specs=[smem, smem, vmem, vmem, vmem, vmem, vmem],
         out_specs=vmem,
         scratch_shapes=[pltpu.VMEM((count, META, LANES), jnp.float32)],
+        compiler_params=pltpu.CompilerParams(vmem_limit_bytes=16 << 20),
         name="pack",
     )(assignment, neighbour, features, diag_blocks, coupling_blocks, feature_drop, edge_drop)
     parity = lax.axis_index("store") % 2
@@ -293,7 +294,7 @@
             pltpu.VMEM((3, count, columns), jnp.float32),
             pltpu.SemaphoreType.DMA,
         ],
-        compiler_params=pltpu.CompilerParams(vmem_limit_bytes=56 << 20),
+        compiler_params=pltpu.CompilerParams(vmem_limit_bytes=46 << 20),
         name="step",
     )(parity.reshape(1).astype(jnp.int32), weights, recv)
 

time: 132 us -> 130 us (0.985)
  Pallas kernels: 30 us -> 23.5 us
  local copies, waits for them, and re-layouts: 0.04 us -> 5.93 us
    unnamed x0 -> x16, local copies, waits for them, and re-layouts: none -> 5.89 us
    pallas_call x1, Pallas kernels: 26.2 us -> 22.3 us  [local(): pl.pallas_call(step_kernel, out_shape=[half, half], in_specs=[smem, vmem,...]
    pallas_call x1, Pallas kernels: 3.73 us -> 1.2 us  [local(): pl.pallas_call(pack_kernel, out_shape=jax.ShapeDtypeStruct((count, body +...]
where the time goes in v4:
time: 130 us; the launch traced here: 129 us
  blocking collectives  89.3 us (69%)
  Pallas kernels  23.5 us (18%)
  local copies, waits for them, and re-layouts  5.93 us (5%)
  starting transfers between devices  4.18 us (3%)
  waiting for transfers between devices  3.82 us (3%)
  other arithmetic  1.84 us (1%)
    all_to_all x1, blocking collectives, local(): lax.all_to_all(send, 'batch', split_axis=0, concat_axis=0, tiled=True)  47.7 us
    all_to_all x1, blocking collectives, local(): lax.all_to_all(kept.reshape(chips, columns // chips, columns), axes, spli...  26.2 us
    pallas_call x1, Pallas kernels, local(): pl.pallas_call(step_kernel, out_shape=[half, half], in_specs=[smem, vmem,...  22.3 us
    all_to_all x1, blocking collectives, local(): lax.all_to_all(jnp.broadcast_to(piece[None], (chips,) + piece.shape), axe...  15.3 us
    unnamed x16, local copies, waits for them, and re-layouts  5.89 us
    ppermute x1, starting transfers between devices, local(): other = lax.ppermute(layer, 'store', swap)  3.15 us
  transfers between devices with their start and end apart: 2, of which 2 were waited for; matrix products, arithmetic and copies ran while one was open for 0% of the time, Pallas kernels for 0%

profile of v4, /device:TPU:1, one launch (start us, length us, event | category | flops | bytes accessed | tf_op | source)
XLA Modules:
  0.0 128.6 jit_solution(8093072042017795887)
XLA Ops:
  0.0 0.0 copy-start.1
  0.0 1.2 copy-done.1
  1.2 0.0 copy-start.2
  1.2 0.9 copy-done.2
  2.2 0.0 copy-start.3
  2.2 0.9 copy-done.3
  3.1 0.0 copy-start.4
  3.1 0.8 copy-done.4
  3.9 0.0 copy-start.5
  3.9 0.7 copy-done.5
  4.6 0.0 copy-start.6
  4.6 0.7 copy-done.6
  5.2 0.0 copy-start.7
  5.2 0.7 copy-done.7
  5.9 1.2 pack.1
  7.1 0.0 copy-start
  7.1 47.7 %all_to_all.15.recv = bf16[16,784,128]{2,1,0:T(8,128)(2,1)S(1)} all-to-all(bf16[16,784,128]{2,1,0:T(8,128)(2,1)S(1)} %pack.1), channel_id=1, replica_groups=mesh['store'=8,'batch'=16] {'batch'}, dimensions={0} | all-to-all | bytes 6422528 | tf_op jit(solution)/shard_map/all_to_all | solution.py:271
  54.8 0.0 copy-done
  54.8 22.3 %step.1 = (f32[512,512]{1,0:T(8,128)S(1)}, f32[512,512]{1,0:T(8,128)S(1)}) custom-call(s32[1]{0:T(128)} %bitcast.core, bf16[2,512,512]{2,1,0:T(8,128)(2,1)S(1)} %copy-done, bf16[16,784,128]{2,1,0:T(8,128)(2,1)S(1)} %all_to_all.15.recv), custom_call_target="tpu_custom_call" | custom-call | tf_op jit(solution)/shard_map/step/pallas_call | solution.py:274
  77.1 1.0 collective-permute-start
  78.1 2.3 %collective-permute-done = f32[512,512]{1,0:T(8,128)S(1)} collective-permute-done((f32[512,512]{1,0:T(8,128)S(1)}, f32[512,512]{1,0:T(8,128)S(1)}, u32[]{:S(2)}, u32[]{:S(2)}) %collective-permute-start) | collective-permute-done | bytes 1048608 | tf_op jit(solution)/shard_map/ppermute | solution.py:302
  80.4 0.2 add_bitcast_fusion
  80.6 26.2 %all_to_all.16 = f32[64,8,512]{2,1,0:T(8,128)S(1)} all-to-all(f32[64,8,512]{2,1,0:T(8,128)S(1)} %add_bitcast_fusion), channel_id=1, replica_groups={{0,1,2,3,4,5,6,7,8,9,10,11,12,13,14,15,32,33,34,35,36,37,38,39,40,41,42..., dimensions={0} | all-to-all | bytes 2097152 | tf_op jit(solution)/shard_map/all_to_all | solution.py:308
  106.9 0.1 reduce_sum.9
  107.0 15.3 %all_to_all.17 = bf16[64,8,512]{2,1,0:T(8,128)(2,1)S(1)} all-to-all(bf16[64,8,512]{2,1,0:T(8,128)(2,1)S(1)} %broadcast_in_dim.2), channel_id=1, replica_groups={{0,1,2,3,4,5,6,7,8,9,10,11,12,13,14,15,32,33,34,35,36,37,38,39,40,41,42..., dimensions={0} | all-to-all | bytes 1048576 | tf_op jit(solution)/shard_map/all_to_all | solution.py:313
  122.3 3.2 %collective-permute-start.1 = (bf16[512,512]{1,0:T(8,128)(2,1)S(1)}, bf16[512,512]{1,0:T(8,128)(2,1)S(1)}, u32[]{:S(2)}, u32[]{:S(2)}) collective-permute-start(bf16[512,512]{1,0:T(8,128)(2,1)S(1)} %bitcast.10), channel_id=1, source_target_pairs={{0,16},{16,0},{32,48},{48,32},{64,80},{80,64},{96,112},{112,96},{1... | collective-permute-start | bytes 1572872 | tf_op jit(solution)/shard_map/ppermute | solution.py:317
  125.5 1.5 %collective-permute-done.1 = bf16[512,512]{1,0:T(8,128)(2,1)S(1)} collective-permute-done((bf16[512,512]{1,0:T(8,128)(2,1)S(1)}, bf16[512,512]{1,0:T(8,128)(2,1)S(1)}, u32[]{:S(2)}, u32[]{:S(2)}) %collective-permute-start.1) | collective-permute-done | bytes 524320 | tf_op jit(solution)/shard_map/ppermute | solution.py:317
  127.0 0.1 select_bitcast_fusion.1
  127.1 1.5 %maximum_convert_fusion = f32[2,512,512]{2,1,0:T(8,128)} fusion(bf16[1,512,512]{2,1,0:T(8,128)(2,1)S(1)} %get-tuple-element.14, bf16[1,512,512]{2,1,0:T(8,128)(2,1)S(1)} %get-tuple-element.13), kind=kLoop, calls=%fused_computation | loop fusion | flops 1048576 | bytes 3145728 | tf_op jit(solution)/shard_map/convert_element_type | solution.py:321
  (1 shorter events, 0.0 us)
Async XLA Ops:
  0.0 1.2 copy-start.1
  1.2 0.9 copy-start.2
  2.2 0.9 copy-start.3
  3.1 0.8 copy-start.4
  3.9 0.7 copy-start.5
  4.6 0.7 copy-start.6
  5.2 0.7 copy-start.7
  7.1 47.7 %copy-start = (bf16[2,512,512]{2,1,0:T(8,128)(2,1)S(1)}, bf16[2,512,512]{2,1,0:T(8,128)(2,1)}, u32[]{:S(2)}) copy-start(bf16[2,512,512]{2,1,0:T(8,128)(2,1)} %weights.1) | copy-start | bytes 3145732
  77.1 3.3 %collective-permute-start = (f32[512,512]{1,0:T(8,128)S(1)}, f32[512,512]{1,0:T(8,128)S(1)}, u32[]{:S(2)}, u32[]{:S(2)}) collective-permute-start(f32[512,512]{1,0:T(8,128)S(1)} %get-tuple-element.12), channel_id=1, source_target_pairs={{0,16},{16,0},{32,48},{48,32},{64,80},{80,64},{96,112},{112,96},{1... | collective-permute-start | bytes 3145736 | tf_op jit(solution)/shard_map/ppermute | solution.py:302
  122.3 4.7 %collective-permute-start.1 = (bf16[512,512]{1,0:T(8,128)(2,1)S(1)}, bf16[512,512]{1,0:T(8,128)(2,1)S(1)}, u32[]{:S(2)}, u32[]{:S(2)}) collective-permute-start(bf16[512,512]{1,0:T(8,128)(2,1)S(1)} %bitcast.10), channel_id=1, source_target_pairs={{0,16},{16,0},{32,48},{48,32},{64,80},{80,64},{96,112},{112,96},{1... | collective-permute-start | bytes 1572872 | tf_op jit(solution)/shard_map/ppermute | solution.py:317

commit v5 on v4

--- a/solution.py
+++ b/solution.py
@@ -11,9 +11,9 @@
 LANES = 128
 META = 16
 UA = 8
-UB = 16
-UC = 16
-CHUNK = 16
+UB = 8
+UC = 8
+UD = 8
 
 
 def pack_kernel(
@@ -49,9 +49,9 @@
 
 
 def step_kernel(
-    core, weights, recv, kept, given,
-    slots, links, first, extra_count, extra_to, extra_from,
-    h0, p0, p1, h1, near, far, active, sums, pooled, link_sem,
+    core, weights, recv, out,
+    slots, links, first, seen, several, further, shared,
+    h0, p0, p1, h1, near, far, active, spread, sums, pooled, link_sem,
 ):
     count = recv.shape[0]
     columns = weights.shape[1]
@@ -59,7 +59,6 @@
     nodes = near.shape[1]
     body = (blocks + 2) * nodes
     rows = 2 * nodes
-    chunk = sums.shape[0] // rows
     low = jnp.bfloat16
 
     slots[...] = recv[:, pl.ds(body, META), :].astype(jnp.float32)
@@ -77,24 +76,26 @@
 
     for s in range(count):
         first[s] = count
-    for i in range(count // chunk):
-        extra_count[i] = 0
+        seen[s] = 0
+    shared[0] = 0
 
     def enlist(s, carry):
         n = links[s, 0]
-        i = n // chunk
-        taken = first[n] != count
-
-        @pl.when(taken)
-        def _():
-            k = extra_count[i]
-            extra_to[i * count + k] = n
-            extra_from[i * count + k] = s
-            extra_count[i] = k + 1
-
-        @pl.when(jnp.logical_not(taken))
+        k = seen[n]
+        seen[n] = k + 1
+
+        @pl.when(k == 0)
         def _():
             first[n] = s
+
+        @pl.when(k > 0)
+        def _():
+            further[n * count + k] = s
+
+        @pl.when(k == 1)
+        def _():
+            several[shared[0]] = n
+            shared[0] = shared[0] + 1
 
         return carry
 
@@ -186,64 +187,47 @@
         )
         pooled[v] = (grad / nodes).astype(low).astype(jnp.float32)
 
-    def add(layer, part_sum):
-        @pl.when(core[0] == layer)
-        def _():
-            kept[...] = kept[...] + part_sum
-
-        @pl.when(core[0] != layer)
-        def _():
-            given[...] = given[...] + part_sum
-
-    kept[...] = jnp.zeros_like(kept)
-    given[...] = jnp.zeros_like(given)
-
-    def spread(i, grad_of):
-        for u in range(chunk):
-            s = i * chunk + u
+    def back(grad_of, hidden, layer):
+        def pull(s, v):
             a = first[s]
             b = jnp.minimum(a, count - 1)
+            return dot(
+                jnp.concatenate([near[2 * s + v], far[2 * a + v]], axis=0),
+                jnp.concatenate([grad_of(s, v), grad_of(b, v)], axis=0),
+                ((0,), (0,)),
+            )
+
+        def straight(s):
             for v in range(2):
-                sums[pl.ds(u * rows + v * nodes, nodes), :] = dot(
-                    jnp.concatenate([near[2 * s + v], far[2 * a + v]], axis=0),
-                    jnp.concatenate([grad_of(s, v), grad_of(b, v)], axis=0),
-                    ((0,), (0,)),
-                )
-
-        def further(k, carry):
-            a = extra_from[i * count + k]
-            u = extra_to[i * count + k] - i * chunk
+                spread[part(s, v), :] = pull(s, v).astype(low)
+
+        each(UD, straight)
+
+        def joined(k, carry):
+            c = several[k]
             for v in range(2):
-                mine = part(u, v)
-                sums[mine, :] = sums[mine, :] + dot(far[2 * a + v], grad_of(a, v), ((0,), (0,)))
+                sums[v] = pull(c, v)
+
+            def more(j, inner):
+                a = further[c * count + j]
+                for v in range(2):
+                    sums[v] = sums[v] + dot(far[2 * a + v], grad_of(a, v), ((0,), (0,)))
+                return inner
+
+            lax.fori_loop(1, seen[c], more, 0)
+            for v in range(2):
+                spread[part(c, v), :] = sums[v].astype(low)
             return carry
 
-        lax.fori_loop(0, extra_count[i], further, 0)
-        return sums[...].astype(low)
-
-    def second_grad(s, v):
-        return active[part(s, v), :] * pooled[v, pl.ds(s, 1), :].astype(low)
-
-    def second_back(i, carry):
-        grad = spread(i, second_grad)
-        span = pl.ds(i * chunk * rows, chunk * rows)
-        hidden = h1[span, :]
-        add(1, dot(hidden, grad, ((0,), (0,))))
-        below = dot(grad, weights[1], ((1,), (1,)))
-        p0[span, :] = jnp.where(hidden > 0, below, 0.0).astype(low)
-        return carry
-
-    lax.fori_loop(0, count // chunk, second_back, 0)
-
-    def first_grad(s, v):
-        return p0[part(s, v), :]
-
-    def first_back(i, carry):
-        grad = spread(i, first_grad)
-        add(0, dot(h0[pl.ds(i * chunk * rows, chunk * rows), :], grad, ((0,), (0,))))
-        return carry
-
-    lax.fori_loop(0, count // chunk, first_back, 0)
+        lax.fori_loop(0, shared[0], joined, 0)
+        out[core[0] ^ layer] = dot(hidden[...], spread[...], ((0,), (0,)))
+
+    back(
+        lambda s, v: active[part(s, v), :] * pooled[v, pl.ds(s, 1), :].astype(low), h1, 1
+    )
+    below = dot(spread[...], weights[1], ((1,), (1,)))
+    p0[...] = jnp.where(h1[...] > 0, below, 0.0).astype(low)
+    back(lambda s, v: p0[part(s, v), :], h0, 0)
 
 
 def local(
@@ -263,26 +247,25 @@
         in_specs=[smem, smem, vmem, vmem, vmem, vmem, vmem],
         out_specs=vmem,
         scratch_shapes=[pltpu.VMEM((count, META, LANES), jnp.float32)],
-        compiler_params=pltpu.CompilerParams(vmem_limit_bytes=16 << 20),
         name="pack",
     )(assignment, neighbour, features, diag_blocks, coupling_blocks, feature_drop, edge_drop)
     parity = lax.axis_index("store") % 2
     send, parity = lax.optimization_barrier((send, parity))
     recv = lax.all_to_all(send, "batch", split_axis=0, concat_axis=0, tiled=True)
     total = count * 2 * nodes
-    half = jax.ShapeDtypeStruct((columns, columns), jnp.float32)
-    kept, given = pl.pallas_call(
+    halves = pl.pallas_call(
         step_kernel,
-        out_shape=[half, half],
+        out_shape=jax.ShapeDtypeStruct((2, columns, columns), jnp.float32),
         in_specs=[smem, vmem, vmem],
-        out_specs=[vmem, vmem],
+        out_specs=vmem,
         scratch_shapes=[
             pltpu.VMEM((count, META, LANES), jnp.float32),
             pltpu.SMEM((count, LANES), jnp.int32),
             pltpu.SMEM((count,), jnp.int32),
             pltpu.SMEM((count,), jnp.int32),
+            pltpu.SMEM((count,), jnp.int32),
             pltpu.SMEM((count * count,), jnp.int32),
-            pltpu.SMEM((count * count,), jnp.int32),
+            pltpu.SMEM((1,), jnp.int32),
             pltpu.VMEM((total, columns), low),
             pltpu.VMEM((total, columns), low),
             pltpu.VMEM((total, columns), low),
@@ -290,7 +273,8 @@
             pltpu.VMEM((2 * count, nodes, nodes), low),
             pltpu.VMEM((2 * count + 2, nodes, nodes), low),
             pltpu.VMEM((total, columns), low),
-            pltpu.VMEM((CHUNK * 2 * nodes, columns), jnp.float32),
+            pltpu.VMEM((total, columns), low),
+            pltpu.VMEM((2, nodes, columns), jnp.float32),
             pltpu.VMEM((3, count, columns), jnp.float32),
             pltpu.SemaphoreType.DMA,
         ],
@@ -299,7 +283,7 @@
     )(parity.reshape(1).astype(jnp.int32), weights, recv)
 
     swap = [(s, s ^ 1) for s in range(stores)]
-    kept = kept + lax.ppermute(given, "store", swap)
+    kept = halves[0] + lax.ppermute(halves[1], "store", swap)
     chips = stores // 2 * count
     groups = [
         [s * count + b for s in range(c, stores, 2) for b in range(count)] for c in range(2)

time: 130 us -> 130 us (level)
  Pallas kernels: 23.5 us -> 31.5 us
  local copies, waits for them, and re-layouts: 5.93 us -> 0.11 us
    unnamed x16 -> x2, local copies, waits for them, and re-layouts: 5.89 us -> 0.01 us
    pallas_call x1, Pallas kernels: 22.3 us -> 27.8 us  [local(): pl.pallas_call(step_kernel, out_shape=jax.ShapeDtypeStruct((2, columns, c...]
    pallas_call x1, Pallas kernels: 1.2 us -> 3.71 us  [local(): pl.pallas_call(pack_kernel, out_shape=jax.ShapeDtypeStruct((count, body +...]
where the time goes in v5:
time: 130 us
  blocking collectives  88.8 us (68%)
  Pallas kernels  31.5 us (24%)
  waiting for transfers between devices  4.18 us (3%)
  starting transfers between devices  3.24 us (2%)
  other arithmetic  1.83 us (1%)
    all_to_all x1, blocking collectives, local(): lax.all_to_all(send, 'batch', split_axis=0, concat_axis=0, tiled=True)  47.9 us
    pallas_call x1, Pallas kernels, local(): pl.pallas_call(step_kernel, out_shape=jax.ShapeDtypeStruct((2, columns, c...  27.8 us
    all_to_all x1, blocking collectives, local(): lax.all_to_all(kept.reshape(chips, columns // chips, columns), axes, spli...  25.6 us
    all_to_all x1, blocking collectives, local(): lax.all_to_all(jnp.broadcast_to(piece[None], (chips,) + piece.shape), axe...  15.3 us
    pallas_call x1, Pallas kernels, local(): pl.pallas_call(pack_kernel, out_shape=jax.ShapeDtypeStruct((count, body +...  3.71 us
    ppermute x1, starting transfers between devices, local(): other = lax.ppermute(layer, 'store', swap)  3.15 us
    ppermute x1, waiting for transfers between devices, local(): kept = halves[0] + lax.ppermute(halves[1], 'store', swap)  2.65 us
  transfers between devices with their start and end apart: 2, of which 2 were waited for; matrix products, arithmetic and copies ran while one was open for 0% of the time, Pallas kernels for 0%

profile of v5, /device:TPU:1, one launch (start us, length us, event | category | flops | bytes accessed | tf_op | source)
XLA Modules:
  0.0 129.7 jit_solution(11764799195740203867)
XLA Ops:
  0.0 3.7 %pack.1 = bf16[16,784,128]{2,1,0:T(8,128)(2,1)} custom-call(s32[1,8]{1,0:T(1,128)} %assign.1, s32[1,8]{1,0:T(1,128)} %neighbour.1, bf16[1,8,128,512]{3,2,1,0:T(8,128)(2,1)} %features.1, bf16[1,8,128,128]{3,2,1,0:T(8,128)(2,1)} %diag.1, bf16[1,8,128,128]{3,2,1,0:T(8,128)(2,1)} %coupling.1, s32[1,8,2,512]{3,2,1,0:T(2,128)} %feature_drop.1, ...), custom_call_target="tpu_custom_call" | custom-call | tf_op jit(solution)/shard_map/pack/pallas_call | solution.py:244
  3.7 0.0 copy-start
  3.7 47.9 %all_to_all.15.recv = bf16[16,784,128]{2,1,0:T(8,128)(2,1)S(1)} all-to-all(bf16[16,784,128]{2,1,0:T(8,128)(2,1)} %pack.1), channel_id=1, replica_groups=mesh['store'=8,'batch'=16] {'batch'}, dimensions={0} | all-to-all | bytes 6422528 | tf_op jit(solution)/shard_map/all_to_all | solution.py:254
  51.6 0.0 copy-done
  51.6 27.8 %step.1 = f32[2,512,512]{2,1,0:T(8,128)S(1)} custom-call(s32[1]{0:T(128)} %bitcast.core, bf16[2,512,512]{2,1,0:T(8,128)(2,1)S(1)} %copy-done, bf16[16,784,128]{2,1,0:T(8,128)(2,1)S(1)} %all_to_all.15.recv), custom_call_target="tpu_custom_call" | custom-call | tf_op jit(solution)/shard_map/step/pallas_call | solution.py:256
  79.4 0.1 slice_bitcast_fusion
  79.5 0.1 collective-permute-start
  79.6 2.6 %collective-permute-done = f32[512,512]{1,0:T(8,128)S(1)} collective-permute-done((f32[512,512]{1,0:T(8,128)S(1)}, f32[512,512]{1,0:T(8,128)S(1)}, u32[]{:S(2)}, u32[]{:S(2)}) %collective-permute-start) | collective-permute-done | bytes 1048608 | tf_op jit(solution)/shard_map/ppermute | solution.py:286
  82.2 0.2 fusion.1
  82.4 25.6 %all_to_all.16 = f32[64,8,512]{2,1,0:T(8,128)S(1)} all-to-all(f32[64,8,512]{2,1,0:T(8,128)S(1)} %fusion.1), channel_id=1, replica_groups={{0,1,2,3,4,5,6,7,8,9,10,11,12,13,14,15,32,33,34,35,36,37,38,39,40,41,42..., dimensions={0} | all-to-all | bytes 2097152 | tf_op jit(solution)/shard_map/all_to_all | solution.py:292
  108.0 0.1 reduce_sum.9
  108.2 15.3 %all_to_all.17 = bf16[64,8,512]{2,1,0:T(8,128)(2,1)S(1)} all-to-all(bf16[64,8,512]{2,1,0:T(8,128)(2,1)S(1)} %broadcast_in_dim.2), channel_id=1, replica_groups={{0,1,2,3,4,5,6,7,8,9,10,11,12,13,14,15,32,33,34,35,36,37,38,39,40,41,42..., dimensions={0} | all-to-all | bytes 1048576 | tf_op jit(solution)/shard_map/all_to_all | solution.py:297
  123.5 3.2 %collective-permute-start.1 = (bf16[512,512]{1,0:T(8,128)(2,1)S(1)}, bf16[512,512]{1,0:T(8,128)(2,1)S(1)}, u32[]{:S(2)}, u32[]{:S(2)}) collective-permute-start(bf16[512,512]{1,0:T(8,128)(2,1)S(1)} %bitcast.18), channel_id=1, source_target_pairs={{0,16},{16,0},{32,48},{48,32},{64,80},{80,64},{96,112},{112,96},{1... | collective-permute-start | bytes 1572872 | tf_op jit(solution)/shard_map/ppermute | solution.py:301
  126.7 1.5 %collective-permute-done.1 = bf16[512,512]{1,0:T(8,128)(2,1)S(1)} collective-permute-done((bf16[512,512]{1,0:T(8,128)(2,1)S(1)}, bf16[512,512]{1,0:T(8,128)(2,1)S(1)}, u32[]{:S(2)}, u32[]{:S(2)}) %collective-permute-start.1) | collective-permute-done | bytes 524320 | tf_op jit(solution)/shard_map/ppermute | solution.py:301
  128.2 0.1 select_bitcast_fusion.1
  128.3 1.5 %maximum_convert_fusion = f32[2,512,512]{2,1,0:T(8,128)} fusion(bf16[1,512,512]{2,1,0:T(8,128)(2,1)S(1)} %get-tuple-element.10, bf16[1,512,512]{2,1,0:T(8,128)(2,1)S(1)} %get-tuple-element.9), kind=kLoop, calls=%fused_computation.4 | loop fusion | flops 1048576 | bytes 3145728 | tf_op jit(solution)/shard_map/convert_element_type | solution.py:305
  (1 shorter events, 0.0 us)
Async XLA Ops:
  3.7 47.9 %copy-start = (bf16[2,512,512]{2,1,0:T(8,128)(2,1)S(1)}, bf16[2,512,512]{2,1,0:T(8,128)(2,1)}, u32[]{:S(2)}) copy-start(bf16[2,512,512]{2,1,0:T(8,128)(2,1)} %weights.1) | copy-start | bytes 3145732
  79.5 2.7 %collective-permute-start = (f32[512,512]{1,0:T(8,128)S(1)}, f32[512,512]{1,0:T(8,128)S(1)}, u32[]{:S(2)}, u32[]{:S(2)}) collective-permute-start(f32[512,512]{1,0:T(8,128)S(1)} %slice_bitcast_fusion), channel_id=1, source_target_pairs={{0,16},{16,0},{32,48},{48,32},{64,80},{80,64},{96,112},{112,96},{1... | collective-permute-start | bytes 3145736 | tf_op jit(solution)/shard_map/ppermute | solution.py:286
  123.5 4.7 %collective-permute-start.1 = (bf16[512,512]{1,0:T(8,128)(2,1)S(1)}, bf16[512,512]{1,0:T(8,128)(2,1)S(1)}, u32[]{:S(2)}, u32[]{:S(2)}) collective-permute-start(bf16[512,512]{1,0:T(8,128)(2,1)S(1)} %bitcast.18), channel_id=1, source_target_pairs={{0,16},{16,0},{32,48},{48,32},{64,80},{80,64},{96,112},{112,96},{1... | collective-permute-start | bytes 1572872 | tf_op jit(solution)/shard_map/ppermute | solution.py:301

commit v6 on v4

--- a/solution.py
+++ b/solution.py
@@ -49,7 +49,7 @@
 
 
 def step_kernel(
-    core, weights, recv, kept, given,
+    core, weights, recv, out,
     slots, links, first, extra_count, extra_to, extra_from,
     h0, p0, p1, h1, near, far, active, sums, pooled, link_sem,
 ):
@@ -186,18 +186,6 @@
         )
         pooled[v] = (grad / nodes).astype(low).astype(jnp.float32)
 
-    def add(layer, part_sum):
-        @pl.when(core[0] == layer)
-        def _():
-            kept[...] = kept[...] + part_sum
-
-        @pl.when(core[0] != layer)
-        def _():
-            given[...] = given[...] + part_sum
-
-    kept[...] = jnp.zeros_like(kept)
-    given[...] = jnp.zeros_like(given)
-
     def spread(i, grad_of):
         for u in range(chunk):
             s = i * chunk + u
@@ -224,26 +212,15 @@
     def second_grad(s, v):
         return active[part(s, v), :] * pooled[v, pl.ds(s, 1), :].astype(low)
 
-    def second_back(i, carry):
-        grad = spread(i, second_grad)
-        span = pl.ds(i * chunk * rows, chunk * rows)
-        hidden = h1[span, :]
-        add(1, dot(hidden, grad, ((0,), (0,))))
-        below = dot(grad, weights[1], ((1,), (1,)))
-        p0[span, :] = jnp.where(hidden > 0, below, 0.0).astype(low)
-        return carry
-
-    lax.fori_loop(0, count // chunk, second_back, 0)
+    grad = spread(0, second_grad)
+    out[core[0] ^ 1] = dot(h1[...], grad, ((0,), (0,)))
+    below = dot(grad, weights[1], ((1,), (1,)))
+    p0[...] = jnp.where(h1[...] > 0, below, 0.0).astype(low)
 
     def first_grad(s, v):
         return p0[part(s, v), :]
 
-    def first_back(i, carry):
-        grad = spread(i, first_grad)
-        add(0, dot(h0[pl.ds(i * chunk * rows, chunk * rows), :], grad, ((0,), (0,))))
-        return carry
-
-    lax.fori_loop(0, count // chunk, first_back, 0)
+    out[core[0]] = dot(h0[...], spread(0, first_grad), ((0,), (0,)))
 
 
 def local(
@@ -263,19 +240,17 @@
         in_specs=[smem, smem, vmem, vmem, vmem, vmem, vmem],
         out_specs=vmem,
         scratch_shapes=[pltpu.VMEM((count, META, LANES), jnp.float32)],
-        compiler_params=pltpu.CompilerParams(vmem_limit_bytes=16 << 20),
         name="pack",
     )(assignment, neighbour, features, diag_blocks, coupling_blocks, feature_drop, edge_drop)
     parity = lax.axis_index("store") % 2
     send, parity = lax.optimization_barrier((send, parity))
     recv = lax.all_to_all(send, "batch", split_axis=0, concat_axis=0, tiled=True)
     total = count * 2 * nodes
-    half = jax.ShapeDtypeStruct((columns, columns), jnp.float32)
-    kept, given = pl.pallas_call(
+    halves = pl.pallas_call(
         step_kernel,
-        out_shape=[half, half],
+        out_shape=jax.ShapeDtypeStruct((2, columns, columns), jnp.float32),
         in_specs=[smem, vmem, vmem],
-        out_specs=[vmem, vmem],
+        out_specs=vmem,
         scratch_shapes=[
             pltpu.VMEM((count, META, LANES), jnp.float32),
             pltpu.SMEM((count, LANES), jnp.int32),
@@ -299,7 +274,7 @@
     )(parity.reshape(1).astype(jnp.int32), weights, recv)
 
     swap = [(s, s ^ 1) for s in range(stores)]
-    kept = kept + lax.ppermute(given, "store", swap)
+    kept = halves[0] + lax.ppermute(halves[1], "store", swap)
     chips = stores // 2 * count
     groups = [
         [s * count + b for s in range(c, stores, 2) for b in range(count)] for c in range(2)

time: 130 us -> 126 us (0.969)
  local copies, waits for them, and re-layouts: 5.93 us -> 0.11 us
  Pallas kernels: 23.5 us -> 25.4 us
    unnamed x16 -> x2, local copies, waits for them, and re-layouts: 5.89 us -> 0.01 us
    pallas_call x1, Pallas kernels: 1.2 us -> 3.7 us  [local(): pl.pallas_call(pack_kernel, out_shape=jax.ShapeDtypeStruct((count, body +...]
where the time goes in v6:
time: 126 us
  blocking collectives  89.4 us (71%)
  Pallas kernels  25.4 us (20%)
  starting transfers between devices  5.19 us (4%)
  waiting for transfers between devices  3.82 us (3%)
  other arithmetic  1.83 us (1%)
    all_to_all x1, blocking collectives, local(): lax.all_to_all(send, 'batch', split_axis=0, concat_axis=0, tiled=True)  47.9 us
    all_to_all x1, blocking collectives, local(): lax.all_to_all(kept.reshape(chips, columns // chips, columns), axes, spli...  26.1 us
    pallas_call x1, Pallas kernels, local(): pl.pallas_call(step_kernel, out_shape=jax.ShapeDtypeStruct((2, columns, c...  21.7 us
    all_to_all x1, blocking collectives, local(): lax.all_to_all(jnp.broadcast_to(piece[None], (chips,) + piece.shape), axe...  15.3 us
    pallas_call x1, Pallas kernels, local(): pl.pallas_call(pack_kernel, out_shape=jax.ShapeDtypeStruct((count, body +...  3.7 us
    ppermute x1, starting transfers between devices, local(): other = lax.ppermute(layer, 'store', swap)  3.15 us
  transfers between devices with their start and end apart: 2, of which 2 were waited for; matrix products, arithmetic and copies ran while one was open for 0% of the time, Pallas kernels for 0%

profile of v6, /device:TPU:1, one launch (start us, length us, event | category | flops | bytes accessed | tf_op | source)
XLA Modules:
  0.0 125.8 jit_solution(11158510128213524956)
XLA Ops:
  0.0 3.7 %pack.1 = bf16[16,784,128]{2,1,0:T(8,128)(2,1)} custom-call(s32[1,8]{1,0:T(1,128)} %assign.1, s32[1,8]{1,0:T(1,128)} %neighbour.1, bf16[1,8,128,512]{3,2,1,0:T(8,128)(2,1)} %features.1, bf16[1,8,128,128]{3,2,1,0:T(8,128)(2,1)} %diag.1, bf16[1,8,128,128]{3,2,1,0:T(8,128)(2,1)} %coupling.1, s32[1,8,2,512]{3,2,1,0:T(2,128)} %feature_drop.1, ...), custom_call_target="tpu_custom_call" | custom-call | tf_op jit(solution)/shard_map/pack/pallas_call | solution.py:237
  3.7 0.0 copy-start
  3.7 47.9 %all_to_all.15.recv = bf16[16,784,128]{2,1,0:T(8,128)(2,1)S(1)} all-to-all(bf16[16,784,128]{2,1,0:T(8,128)(2,1)} %pack.1), channel_id=1, replica_groups=mesh['store'=8,'batch'=16] {'batch'}, dimensions={0} | all-to-all | bytes 6422528 | tf_op jit(solution)/shard_map/all_to_all | solution.py:247
  51.6 0.0 copy-done
  51.6 21.7 %step.1 = f32[2,512,512]{2,1,0:T(8,128)S(1)} custom-call(s32[1]{0:T(128)} %bitcast.core, bf16[2,512,512]{2,1,0:T(8,128)(2,1)S(1)} %copy-done, bf16[16,784,128]{2,1,0:T(8,128)(2,1)S(1)} %all_to_all.15.recv), custom_call_target="tpu_custom_call" | custom-call | tf_op jit(solution)/shard_map/step/pallas_call | solution.py:249
  73.4 0.1 slice_bitcast_fusion
  73.4 2.0 %collective-permute-start = (f32[512,512]{1,0:T(8,128)S(1)}, f32[512,512]{1,0:T(8,128)S(1)}, u32[]{:S(2)}, u32[]{:S(2)}) collective-permute-start(f32[512,512]{1,0:T(8,128)S(1)} %slice_bitcast_fusion), channel_id=1, source_target_pairs={{0,16},{16,0},{32,48},{48,32},{64,80},{80,64},{96,112},{112,96},{1... | collective-permute-start | bytes 3145736 | tf_op jit(solution)/shard_map/ppermute | solution.py:277
  75.5 2.3 %collective-permute-done = f32[512,512]{1,0:T(8,128)S(1)} collective-permute-done((f32[512,512]{1,0:T(8,128)S(1)}, f32[512,512]{1,0:T(8,128)S(1)}, u32[]{:S(2)}, u32[]{:S(2)}) %collective-permute-start) | collective-permute-done | bytes 1048608 | tf_op jit(solution)/shard_map/ppermute | solution.py:277
  77.8 0.2 fusion.1
  78.0 26.1 %all_to_all.16 = f32[64,8,512]{2,1,0:T(8,128)S(1)} all-to-all(f32[64,8,512]{2,1,0:T(8,128)S(1)} %fusion.1), channel_id=1, replica_groups={{0,1,2,3,4,5,6,7,8,9,10,11,12,13,14,15,32,33,34,35,36,37,38,39,40,41,42..., dimensions={0} | all-to-all | bytes 2097152 | tf_op jit(solution)/shard_map/all_to_all | solution.py:283
  104.1 0.1 reduce_sum.9
  104.2 15.3 %all_to_all.17 = bf16[64,8,512]{2,1,0:T(8,128)(2,1)S(1)} all-to-all(bf16[64,8,512]{2,1,0:T(8,128)(2,1)S(1)} %broadcast_in_dim.2), channel_id=1, replica_groups={{0,1,2,3,4,5,6,7,8,9,10,11,12,13,14,15,32,33,34,35,36,37,38,39,40,41,42..., dimensions={0} | all-to-all | bytes 1048576 | tf_op jit(solution)/shard_map/all_to_all | solution.py:288
  119.6 3.2 %collective-permute-start.1 = (bf16[512,512]{1,0:T(8,128)(2,1)S(1)}, bf16[512,512]{1,0:T(8,128)(2,1)S(1)}, u32[]{:S(2)}, u32[]{:S(2)}) collective-permute-start(bf16[512,512]{1,0:T(8,128)(2,1)S(1)} %bitcast.18), channel_id=1, source_target_pairs={{0,16},{16,0},{32,48},{48,32},{64,80},{80,64},{96,112},{112,96},{1... | collective-permute-start | bytes 1572872 | tf_op jit(solution)/shard_map/ppermute | solution.py:292
  122.7 1.5 %collective-permute-done.1 = bf16[512,512]{1,0:T(8,128)(2,1)S(1)} collective-permute-done((bf16[512,512]{1,0:T(8,128)(2,1)S(1)}, bf16[512,512]{1,0:T(8,128)(2,1)S(1)}, u32[]{:S(2)}, u32[]{:S(2)}) %collective-permute-start.1) | collective-permute-done | bytes 524320 | tf_op jit(solution)/shard_map/ppermute | solution.py:292
  124.3 0.1 select_bitcast_fusion.1
  124.3 1.5 %maximum_convert_fusion = f32[2,512,512]{2,1,0:T(8,128)} fusion(bf16[1,512,512]{2,1,0:T(8,128)(2,1)S(1)} %get-tuple-element.10, bf16[1,512,512]{2,1,0:T(8,128)(2,1)S(1)} %get-tuple-element.9), kind=kLoop, calls=%fused_computation.4 | loop fusion | flops 1048576 | bytes 3145728 | tf_op jit(solution)/shard_map/convert_element_type | solution.py:296
  (1 shorter events, 0.0 us)
Async XLA Ops:
  3.7 47.9 %copy-start = (bf16[2,512,512]{2,1,0:T(8,128)(2,1)S(1)}, bf16[2,512,512]{2,1,0:T(8,128)(2,1)}, u32[]{:S(2)}) copy-start(bf16[2,512,512]{2,1,0:T(8,128)(2,1)} %weights.1) | copy-start | bytes 3145732
  73.4 4.3 %collective-permute-start = (f32[512,512]{1,0:T(8,128)S(1)}, f32[512,512]{1,0:T(8,128)S(1)}, u32[]{:S(2)}, u32[]{:S(2)}) collective-permute-start(f32[512,512]{1,0:T(8,128)S(1)} %slice_bitcast_fusion), channel_id=1, source_target_pairs={{0,16},{16,0},{32,48},{48,32},{64,80},{80,64},{96,112},{112,96},{1... | collective-permute-start | bytes 3145736 | tf_op jit(solution)/shard_map/ppermute | solution.py:277
  119.6 4.7 %collective-permute-start.1 = (bf16[512,512]{1,0:T(8,128)(2,1)S(1)}, bf16[512,512]{1,0:T(8,128)(2,1)S(1)}, u32[]{:S(2)}, u32[]{:S(2)}) collective-permute-start(bf16[512,512]{1,0:T(8,128)(2,1)S(1)} %bitcast.18), channel_id=1, source_target_pairs={{0,16},{16,0},{32,48},{48,32},{64,80},{80,64},{96,112},{112,96},{1... | collective-permute-start | bytes 1572872 | tf_op jit(solution)/shard_map/ppermute | solution.py:292

commit v7 on v6

--- a/solution.py
+++ b/solution.py
@@ -14,6 +14,7 @@
 UB = 16
 UC = 16
 CHUNK = 16
+EXTRA = 4
 
 
 def pack_kernel(
@@ -99,6 +100,10 @@
         return carry
 
     lax.fori_loop(0, count, enlist, 0)
+    for i in range(count // chunk):
+        for d in range(EXTRA - 1):
+            extra_to[i * count + extra_count[i] + d] = i * chunk
+            extra_from[i * count + extra_count[i] + d] = count
     far[pl.ds(2 * count, 2)] = jnp.zeros((2, nodes, nodes), low)
 
     def each(width, stage, then=None):
@@ -198,15 +203,20 @@
                     ((0,), (0,)),
                 )
 
-        def further(k, carry):
-            a = extra_from[i * count + k]
-            u = extra_to[i * count + k] - i * chunk
-            for v in range(2):
-                mine = part(u, v)
-                sums[mine, :] = sums[mine, :] + dot(far[2 * a + v], grad_of(a, v), ((0,), (0,)))
+        def further(t, carry):
+            parts = []
+            for d in range(EXTRA):
+                k = i * count + t * EXTRA + d
+                a = extra_from[k]
+                b = jnp.minimum(a, count - 1)
+                for v in range(2):
+                    mine = part(extra_to[k] - i * chunk, v)
+                    parts.append((mine, dot(far[2 * a + v], grad_of(b, v), ((0,), (0,)))))
+            for mine, more in parts:
+                sums[mine, :] = sums[mine, :] + more
             return carry
 
-        lax.fori_loop(0, extra_count[i], further, 0)
+        lax.fori_loop(0, (extra_count[i] + EXTRA - 1) // EXTRA, further, 0)
         return sums[...].astype(low)
 
     def second_grad(s, v):
@@ -256,8 +266,8 @@
             pltpu.SMEM((count, LANES), jnp.int32),
             pltpu.SMEM((count,), jnp.int32),
             pltpu.SMEM((count,), jnp.int32),
-            pltpu.SMEM((count * count,), jnp.int32),
-            pltpu.SMEM((count * count,), jnp.int32),
+            pltpu.SMEM((2 * count * count,), jnp.int32),
+            pltpu.SMEM((2 * count * count,), jnp.int32),
             pltpu.VMEM((total, columns), low),
             pltpu.VMEM((total, columns), low),
             pltpu.VMEM((total, columns), low),

time: 126 us -> 124 us (0.984)
  blocking collectives: 89.4 us -> 87.7 us
    all_to_all x1, blocking collectives: 26.1 us -> 24.5 us  [local(): lax.all_to_all(kept.reshape(chips, columns // chips, columns), axes, spli...]
where the time goes in v7:
time: 124 us
  blocking collectives  87.7 us (71%)
  Pallas kernels  26.3 us (21%)
  starting transfers between devices  4.26 us (3%)
  waiting for transfers between devices  3.82 us (3%)
  other arithmetic  1.83 us (1%)
    all_to_all x1, blocking collectives, local(): lax.all_to_all(send, 'batch', split_axis=0, concat_axis=0, tiled=True)  47.9 us
    all_to_all x1, blocking collectives, local(): lax.all_to_all(kept.reshape(chips, columns // chips, columns), axes, spli...  24.5 us
    pallas_call x1, Pallas kernels, local(): pl.pallas_call(step_kernel, out_shape=jax.ShapeDtypeStruct((2, columns, c...  22.6 us
    all_to_all x1, blocking collectives, local(): lax.all_to_all(jnp.broadcast_to(piece[None], (chips,) + piece.shape), axe...  15.3 us
    pallas_call x1, Pallas kernels, local(): pl.pallas_call(pack_kernel, out_shape=jax.ShapeDtypeStruct((count, body +...  3.71 us
    ppermute x1, starting transfers between devices, local(): other = lax.ppermute(layer, 'store', swap)  3.15 us
  transfers between devices with their start and end apart: 2, of which 2 were waited for; matrix products, arithmetic and copies ran while one was open for 0% of the time, Pallas kernels for 0%

profile of v7, /device:TPU:1, one launch (start us, length us, event | category | flops | bytes accessed | tf_op | source)
XLA Modules:
  0.0 124.1 jit_solution(8237347729374970045)
XLA Ops:
  0.0 3.7 %pack.1 = bf16[16,784,128]{2,1,0:T(8,128)(2,1)} custom-call(s32[1,8]{1,0:T(1,128)} %assign.1, s32[1,8]{1,0:T(1,128)} %neighbour.1, bf16[1,8,128,512]{3,2,1,0:T(8,128)(2,1)} %features.1, bf16[1,8,128,128]{3,2,1,0:T(8,128)(2,1)} %diag.1, bf16[1,8,128,128]{3,2,1,0:T(8,128)(2,1)} %coupling.1, s32[1,8,2,512]{3,2,1,0:T(2,128)} %feature_drop.1, ...), custom_call_target="tpu_custom_call" | custom-call | tf_op jit(solution)/shard_map/pack/pallas_call | solution.py:247
  3.7 0.0 copy-start
  3.7 47.9 %all_to_all.15.recv = bf16[16,784,128]{2,1,0:T(8,128)(2,1)S(1)} all-to-all(bf16[16,784,128]{2,1,0:T(8,128)(2,1)} %pack.1), channel_id=1, replica_groups=mesh['store'=8,'batch'=16] {'batch'}, dimensions={0} | all-to-all | bytes 6422528 | tf_op jit(solution)/shard_map/all_to_all | solution.py:257
  51.6 0.0 copy-done
  51.6 22.6 %step.1 = f32[2,512,512]{2,1,0:T(8,128)S(1)} custom-call(s32[1]{0:T(128)} %bitcast.core, bf16[2,512,512]{2,1,0:T(8,128)(2,1)S(1)} %copy-done, bf16[16,784,128]{2,1,0:T(8,128)(2,1)S(1)} %all_to_all.15.recv), custom_call_target="tpu_custom_call" | custom-call | tf_op jit(solution)/shard_map/step/pallas_call | solution.py:259
  74.2 0.1 slice_bitcast_fusion
  74.3 1.1 collective-permute-start
  75.4 2.3 %collective-permute-done = f32[512,512]{1,0:T(8,128)S(1)} collective-permute-done((f32[512,512]{1,0:T(8,128)S(1)}, f32[512,512]{1,0:T(8,128)S(1)}, u32[]{:S(2)}, u32[]{:S(2)}) %collective-permute-start) | collective-permute-done | bytes 1048608 | tf_op jit(solution)/shard_map/ppermute | solution.py:287
  77.7 0.2 fusion.1
  77.9 24.5 %all_to_all.16 = f32[64,8,512]{2,1,0:T(8,128)S(1)} all-to-all(f32[64,8,512]{2,1,0:T(8,128)S(1)} %fusion.1), channel_id=1, replica_groups={{0,1,2,3,4,5,6,7,8,9,10,11,12,13,14,15,32,33,34,35,36,37,38,39,40,41,42..., dimensions={0} | all-to-all | bytes 2097152 | tf_op jit(solution)/shard_map/all_to_all | solution.py:293
  102.4 0.1 reduce_sum.9
  102.5 15.3 %all_to_all.17 = bf16[64,8,512]{2,1,0:T(8,128)(2,1)S(1)} all-to-all(bf16[64,8,512]{2,1,0:T(8,128)(2,1)S(1)} %broadcast_in_dim.2), channel_id=1, replica_groups={{0,1,2,3,4,5,6,7,8,9,10,11,12,13,14,15,32,33,34,35,36,37,38,39,40,41,42..., dimensions={0} | all-to-all | bytes 1048576 | tf_op jit(solution)/shard_map/all_to_all | solution.py:298
  117.9 3.2 %collective-permute-start.1 = (bf16[512,512]{1,0:T(8,128)(2,1)S(1)}, bf16[512,512]{1,0:T(8,128)(2,1)S(1)}, u32[]{:S(2)}, u32[]{:S(2)}) collective-permute-start(bf16[512,512]{1,0:T(8,128)(2,1)S(1)} %bitcast.18), channel_id=1, source_target_pairs={{0,16},{16,0},{32,48},{48,32},{64,80},{80,64},{96,112},{112,96},{1... | collective-permute-start | bytes 1572872 | tf_op jit(solution)/shard_map/ppermute | solution.py:302
  121.0 1.5 %collective-permute-done.1 = bf16[512,512]{1,0:T(8,128)(2,1)S(1)} collective-permute-done((bf16[512,512]{1,0:T(8,128)(2,1)S(1)}, bf16[512,512]{1,0:T(8,128)(2,1)S(1)}, u32[]{:S(2)}, u32[]{:S(2)}) %collective-permute-start.1) | collective-permute-done | bytes 524320 | tf_op jit(solution)/shard_map/ppermute | solution.py:302
  122.5 0.1 select_bitcast_fusion.1
  122.6 1.5 %maximum_convert_fusion = f32[2,512,512]{2,1,0:T(8,128)} fusion(bf16[1,512,512]{2,1,0:T(8,128)(2,1)S(1)} %get-tuple-element.10, bf16[1,512,512]{2,1,0:T(8,128)(2,1)S(1)} %get-tuple-element.9), kind=kLoop, calls=%fused_computation.4 | loop fusion | flops 1048576 | bytes 3145728 | tf_op jit(solution)/shard_map/convert_element_type | solution.py:306
  (1 shorter events, 0.0 us)
Async XLA Ops:
  3.7 47.9 %copy-start = (bf16[2,512,512]{2,1,0:T(8,128)(2,1)S(1)}, bf16[2,512,512]{2,1,0:T(8,128)(2,1)}, u32[]{:S(2)}) copy-start(bf16[2,512,512]{2,1,0:T(8,128)(2,1)} %weights.1) | copy-start | bytes 3145732
  74.3 3.4 %collective-permute-start = (f32[512,512]{1,0:T(8,128)S(1)}, f32[512,512]{1,0:T(8,128)S(1)}, u32[]{:S(2)}, u32[]{:S(2)}) collective-permute-start(f32[512,512]{1,0:T(8,128)S(1)} %slice_bitcast_fusion), channel_id=1, source_target_pairs={{0,16},{16,0},{32,48},{48,32},{64,80},{80,64},{96,112},{112,96},{1... | collective-permute-start | bytes 3145736 | tf_op jit(solution)/shard_map/ppermute | solution.py:287
  117.9 4.7 %collective-permute-start.1 = (bf16[512,512]{1,0:T(8,128)(2,1)S(1)}, bf16[512,512]{1,0:T(8,128)(2,1)S(1)}, u32[]{:S(2)}, u32[]{:S(2)}) collective-permute-start(bf16[512,512]{1,0:T(8,128)(2,1)S(1)} %bitcast.18), channel_id=1, source_target_pairs={{0,16},{16,0},{32,48},{48,32},{64,80},{80,64},{96,112},{112,96},{1... | collective-permute-start | bytes 1572872 | tf_op jit(solution)/shard_map/ppermute | solution.py:302

commit v8 on v7

--- a/solution.py
+++ b/solution.py
@@ -18,29 +18,78 @@
 
 
 def pack_kernel(
-    assign, neighbour, features, diag, coupling, feature_drop, edge_drop, send, meta
+    assign, neighbour, features, diag, coupling, feature_drop, edge_drop, send,
+    targets, links, used, rows, kept_features, kept_edges, meta, staged, sems, block_sems, out_sems,
 ):
     owned, nodes, columns = features.shape[1:]
+    count = send.shape[0]
     blocks = columns // LANES
+    loads = [
+        pltpu.make_async_copy(source, place, sems.at[i])
+        for i, (source, place) in enumerate(
+            [
+                (assign, targets),
+                (neighbour, links),
+                (feature_drop, kept_features),
+                (edge_drop, kept_edges),
+            ]
+        )
+    ]
+    loads += [
+        pltpu.make_async_copy(features.at[0, k], rows.at[k], sems.at[4 + k]) for k in range(owned)
+    ]
+    for load in loads:
+        load.start()
     meta[...] = jnp.zeros_like(meta)
-    send[:, pl.ds(0, (blocks + 2) * nodes), :] = jnp.zeros(
-        (send.shape[0], (blocks + 2) * nodes, LANES), jnp.bfloat16
-    )
+    for s in range(count):
+        used[s] = 0
+    loads[0].wait()
+    block_loads = []
     for k in range(owned):
-        target = assign[0, k]
-        for j in range(blocks):
-            send[target, pl.ds(j * nodes, nodes), :] = features[0, k, :, pl.ds(j * LANES, LANES)]
-        send[target, pl.ds(blocks * nodes, nodes), :] = diag[0, k]
-        send[target, pl.ds((blocks + 1) * nodes, nodes), :] = coupling[0, k]
+        target = targets[0, k]
+        used[target] = 1
+        for i, source in enumerate((diag, coupling)):
+            load = pltpu.make_async_copy(
+                source.at[0, k],
+                staged.at[target, pl.ds((blocks + i) * nodes, nodes), :],
+                block_sems.at[k, i],
+            )
+            load.start()
+            block_loads.append(load)
+    for load in loads[1:4]:
+        load.wait()
+    for k in range(owned):
+        target = targets[0, k]
         for v in range(2):
             for j in range(blocks):
-                meta[target, v * blocks + j, :] = feature_drop[
+                meta[target, v * blocks + j, :] = kept_features[
                     0, k, v, pl.ds(j * LANES, LANES)
                 ].astype(jnp.float32)
-            meta[target, 2 * blocks + v, :] = edge_drop[0, k, v, :].astype(jnp.float32)
-        slot = neighbour[0, k] // owned + 1
+            meta[target, 2 * blocks + v, :] = kept_edges[0, k, v, :].astype(jnp.float32)
+        slot = links[0, k] // owned + 1
         meta[target, 2 * blocks + 2, :] = jnp.full((LANES,), slot, jnp.float32)
-    send[:, pl.ds((blocks + 2) * nodes, META), :] = meta[...].astype(jnp.bfloat16)
+    staged[:, pl.ds((blocks + 2) * nodes, META), :] = meta[...].astype(jnp.bfloat16)
+
+    def leave(s):
+        return pltpu.make_async_copy(staged.at[s], send.at[s], out_sems.at[s])
+
+    for s in range(count):
+
+        @pl.when(used[s] == 0)
+        def _():
+            staged[s] = jnp.zeros(staged.shape[1:], jnp.bfloat16)
+            leave(s).start()
+
+    for k in range(owned):
+        target = targets[0, k]
+        loads[4 + k].wait()
+        for j in range(blocks):
+            staged[target, pl.ds(j * nodes, nodes), :] = rows[k, :, pl.ds(j * LANES, LANES)]
+        block_loads[2 * k].wait()
+        block_loads[2 * k + 1].wait()
+        leave(target).start()
+    for s in range(count):
+        leave(s).wait()
 
 
 def dot(a, b, contract, precision=None):
@@ -244,12 +293,25 @@
     low = jnp.bfloat16
     smem = pl.BlockSpec(memory_space=pltpu.SMEM)
     vmem = pl.BlockSpec(memory_space=pltpu.VMEM)
+    raw = pl.BlockSpec(memory_space=pl.ANY)
     send = pl.pallas_call(
         pack_kernel,
         out_shape=jax.ShapeDtypeStruct((count, body + META, LANES), low),
-        in_specs=[smem, smem, vmem, vmem, vmem, vmem, vmem],
-        out_specs=vmem,
-        scratch_shapes=[pltpu.VMEM((count, META, LANES), jnp.float32)],
+        in_specs=[raw] * 7,
+        out_specs=raw,
+        scratch_shapes=[
+            pltpu.SMEM((1, owned), jnp.int32),
+            pltpu.SMEM((1, owned), jnp.int32),
+            pltpu.SMEM((count,), jnp.int32),
+            pltpu.VMEM((owned, nodes, columns), low),
+            pltpu.VMEM(feature_drop.shape, jnp.int32),
+            pltpu.VMEM(edge_drop.shape, jnp.int32),
+            pltpu.VMEM((count, META, LANES), jnp.float32),
+            pltpu.VMEM((count, body + META, LANES), low),
+            pltpu.SemaphoreType.DMA((4 + owned,)),
+            pltpu.SemaphoreType.DMA((owned, 2)),
+            pltpu.SemaphoreType.DMA((count,)),
+        ],
         name="pack",
     )(assignment, neighbour, features, diag_blocks, coupling_blocks, feature_drop, edge_drop)
     parity = lax.axis_index("store") % 2

time: 124 us -> 125 us (level)
  starting transfers between devices: 4.26 us -> 6.11 us
  Pallas kernels: 26.3 us -> 24.8 us
    ppermute x1, starting transfers between devices: 1.11 us -> 2.96 us  [local(): kept = halves[0] + lax.ppermute(halves[1], 'store', swap)]
where the time goes in v8:
time: 125 us; the launch traced here: 124 us
  blocking collectives  87.8 us (70%)
  Pallas kernels  24.8 us (20%)
  starting transfers between devices  6.11 us (5%)
  waiting for transfers between devices  3.82 us (3%)
  other arithmetic  1.83 us (1%)
    all_to_all x1, blocking collectives, local(): lax.all_to_all(send, 'batch', split_axis=0, concat_axis=0, tiled=True)  47.9 us
    all_to_all x1, blocking collectives, local(): lax.all_to_all(kept.reshape(chips, columns // chips, columns), axes, spli...  24.5 us
    pallas_call x1, Pallas kernels, local(): pl.pallas_call(step_kernel, out_shape=jax.ShapeDtypeStruct((2, columns, c...  21.7 us
    all_to_all x1, blocking collectives, local(): lax.all_to_all(jnp.broadcast_to(piece[None], (chips,) + piece.shape), axe...  15.3 us
    ppermute x1, starting transfers between devices, local(): other = lax.ppermute(layer, 'store', swap)  3.15 us
    pallas_call x1, Pallas kernels, local(): pl.pallas_call(pack_kernel, out_shape=jax.ShapeDtypeStruct((count, body +...  3.1 us
    ppermute x1, starting transfers between devices, local(): kept = halves[0] + lax.ppermute(halves[1], 'store', swap)  2.96 us
  transfers between devices with their start and end apart: 2, of which 2 were waited for; matrix products, arithmetic and copies ran while one was open for 0% of the time, Pallas kernels for 0%

profile of v8, /device:TPU:1, one launch (start us, length us, event | category | flops | bytes accessed | tf_op | source)
XLA Modules:
  0.0 124.5 jit_solution(9136205145844882855)
XLA Ops:
  0.0 3.1 %pack.1 = bf16[16,784,128]{2,1,0:T(8,128)(2,1)} custom-call(s32[1,8]{1,0:T(1,128)} %assign.1, s32[1,8]{1,0:T(1,128)} %neighbour.1, bf16[1,8,128,512]{3,2,1,0:T(8,128)(2,1)} %features.1, bf16[1,8,128,128]{3,2,1,0:T(8,128)(2,1)} %diag.1, bf16[1,8,128,128]{3,2,1,0:T(8,128)(2,1)} %coupling.1, s32[1,8,2,512]{3,2,1,0:T(2,128)} %feature_drop.1, ...), custom_call_target="tpu_custom_call" | custom-call | tf_op jit(solution)/shard_map/pack/pallas_call | solution.py:297
  3.1 0.0 copy-start
  3.1 47.9 %all_to_all.15.recv = bf16[16,784,128]{2,1,0:T(8,128)(2,1)S(1)} all-to-all(bf16[16,784,128]{2,1,0:T(8,128)(2,1)} %pack.1), channel_id=1, replica_groups=mesh['store'=8,'batch'=16] {'batch'}, dimensions={0} | all-to-all | bytes 6422528 | tf_op jit(solution)/shard_map/all_to_all | solution.py:319
  51.1 0.0 copy-done
  51.1 21.7 %step.1 = f32[2,512,512]{2,1,0:T(8,128)S(1)} custom-call(s32[1]{0:T(128)} %bitcast.core, bf16[2,512,512]{2,1,0:T(8,128)(2,1)S(1)} %copy-done, bf16[16,784,128]{2,1,0:T(8,128)(2,1)S(1)} %all_to_all.15.recv), custom_call_target="tpu_custom_call" | custom-call | tf_op jit(solution)/shard_map/step/pallas_call | solution.py:321
  72.7 0.1 slice_bitcast_fusion
  72.8 3.0 %collective-permute-start = (f32[512,512]{1,0:T(8,128)S(1)}, f32[512,512]{1,0:T(8,128)S(1)}, u32[]{:S(2)}, u32[]{:S(2)}) collective-permute-start(f32[512,512]{1,0:T(8,128)S(1)} %slice_bitcast_fusion), channel_id=1, source_target_pairs={{0,16},{16,0},{32,48},{48,32},{64,80},{80,64},{96,112},{112,96},{1... | collective-permute-start | bytes 3145736 | tf_op jit(solution)/shard_map/ppermute | solution.py:349
  75.8 2.3 %collective-permute-done = f32[512,512]{1,0:T(8,128)S(1)} collective-permute-done((f32[512,512]{1,0:T(8,128)S(1)}, f32[512,512]{1,0:T(8,128)S(1)}, u32[]{:S(2)}, u32[]{:S(2)}) %collective-permute-start) | collective-permute-done | bytes 1048608 | tf_op jit(solution)/shard_map/ppermute | solution.py:349
  78.1 0.2 fusion.1
  78.3 24.5 %all_to_all.16 = f32[64,8,512]{2,1,0:T(8,128)S(1)} all-to-all(f32[64,8,512]{2,1,0:T(8,128)S(1)} %fusion.1), channel_id=1, replica_groups={{0,1,2,3,4,5,6,7,8,9,10,11,12,13,14,15,32,33,34,35,36,37,38,39,40,41,42..., dimensions={0} | all-to-all | bytes 2097152 | tf_op jit(solution)/shard_map/all_to_all | solution.py:355
  102.8 0.1 reduce_sum.9
  102.9 15.3 %all_to_all.17 = bf16[64,8,512]{2,1,0:T(8,128)(2,1)S(1)} all-to-all(bf16[64,8,512]{2,1,0:T(8,128)(2,1)S(1)} %broadcast_in_dim.2), channel_id=1, replica_groups={{0,1,2,3,4,5,6,7,8,9,10,11,12,13,14,15,32,33,34,35,36,37,38,39,40,41,42..., dimensions={0} | all-to-all | bytes 1048576 | tf_op jit(solution)/shard_map/all_to_all | solution.py:360
  118.2 3.2 %collective-permute-start.1 = (bf16[512,512]{1,0:T(8,128)(2,1)S(1)}, bf16[512,512]{1,0:T(8,128)(2,1)S(1)}, u32[]{:S(2)}, u32[]{:S(2)}) collective-permute-start(bf16[512,512]{1,0:T(8,128)(2,1)S(1)} %bitcast.18), channel_id=1, source_target_pairs={{0,16},{16,0},{32,48},{48,32},{64,80},{80,64},{96,112},{112,96},{1... | collective-permute-start | bytes 1572872 | tf_op jit(solution)/shard_map/ppermute | solution.py:364
  121.4 1.5 %collective-permute-done.1 = bf16[512,512]{1,0:T(8,128)(2,1)S(1)} collective-permute-done((bf16[512,512]{1,0:T(8,128)(2,1)S(1)}, bf16[512,512]{1,0:T(8,128)(2,1)S(1)}, u32[]{:S(2)}, u32[]{:S(2)}) %collective-permute-start.1) | collective-permute-done | bytes 524320 | tf_op jit(solution)/shard_map/ppermute | solution.py:364
  122.9 0.1 select_bitcast_fusion.1
  123.0 1.5 %maximum_convert_fusion = f32[2,512,512]{2,1,0:T(8,128)} fusion(bf16[1,512,512]{2,1,0:T(8,128)(2,1)S(1)} %get-tuple-element.10, bf16[1,512,512]{2,1,0:T(8,128)(2,1)S(1)} %get-tuple-element.9), kind=kLoop, calls=%fused_computation.4 | loop fusion | flops 1048576 | bytes 3145728 | tf_op jit(solution)/shard_map/convert_element_type | solution.py:368
  (1 shorter events, 0.0 us)
Async XLA Ops:
  3.1 47.9 %copy-start = (bf16[2,512,512]{2,1,0:T(8,128)(2,1)S(1)}, bf16[2,512,512]{2,1,0:T(8,128)(2,1)}, u32[]{:S(2)}) copy-start(bf16[2,512,512]{2,1,0:T(8,128)(2,1)} %weights.1) | copy-start | bytes 3145732
  72.8 5.2 %collective-permute-start = (f32[512,512]{1,0:T(8,128)S(1)}, f32[512,512]{1,0:T(8,128)S(1)}, u32[]{:S(2)}, u32[]{:S(2)}) collective-permute-start(f32[512,512]{1,0:T(8,128)S(1)} %slice_bitcast_fusion), channel_id=1, source_target_pairs={{0,16},{16,0},{32,48},{48,32},{64,80},{80,64},{96,112},{112,96},{1... | collective-permute-start | bytes 3145736 | tf_op jit(solution)/shard_map/ppermute | solution.py:349
  118.2 4.7 %collective-permute-start.1 = (bf16[512,512]{1,0:T(8,128)(2,1)S(1)}, bf16[512,512]{1,0:T(8,128)(2,1)S(1)}, u32[]{:S(2)}, u32[]{:S(2)}) collective-permute-start(bf16[512,512]{1,0:T(8,128)(2,1)S(1)} %bitcast.18), channel_id=1, source_target_pairs={{0,16},{16,0},{32,48},{48,32},{64,80},{80,64},{96,112},{112,96},{1... | collective-permute-start | bytes 1572872 | tf_op jit(solution)/shard_map/ppermute | solution.py:364
